TPU v7x, 256 devices: a whole 4x4x8 slice. The times are simulated.
256 devices in a mesh: sx: 8 (over y, core), sy: 4 (over z_hi), row: 8 (over x, z_lo).
Axes of the slice: x: 4, y: 4, z: 8 (z_hi: 4, z_lo: 2; z = z_hi * 2 + z_lo), core: 2. Of those that a mesh axis runs over, the one named last changes fastest.
Arguments:
- thermal_state: float32 [256, 512, 512], P('row', 'sx', 'sy'), may hold values from -6 to 6
- substance_label: int32 [256, 512, 512], P('row', 'sx', 'sy'), may hold values from 0 to 2
- thermal_coefficients: float32 [3], replicated, may hold values from 0.04 to 0.16
- optical_thickness: float32 [3], replicated, may hold values from 1 to 6
- substance_colours: float32 [3, 3], replicated, may hold values from 0.1 to 1
Outputs:
- advanced_thermal_state: float32 [256, 512, 512], P('row', 'sx', 'sy')
- output_picture: float32 [4, 512, 512], P(None, ('sx', 'row'), 'sy')
All inputs are finite; a program needn't handle non-finite values.
Results may differ from a plain program's by a relative error of at most 0.00002.
Values sent between devices are 32-bit elements; how exact they have to be, the bound alone decides.
A program may use at most 64 MiB of HBM per device.

v0:
```python
import jax
import jax.numpy as jnp
from jax import lax
from jax.sharding import PartitionSpec as P


def padded(cells, sides, width, closed):
    for axis, dim in sides:
        count = lax.axis_size(axis)
        ends = count if closed else count - 1
        head = lax.slice_in_dim(cells, 0, width, axis=dim)
        tail = lax.slice_in_dim(cells, cells.shape[dim] - width, cells.shape[dim], axis=dim)
        cells = jnp.concatenate(
            [
                lax.ppermute(tail, axis, [(i, (i + 1) % count) for i in range(ends)]),
                cells,
                lax.ppermute(head, axis, [((i + 1) % count, i) for i in range(ends)]),
            ],
            axis=dim,
        )
    return cells


def partner(block, axis, apart):
    count = lax.axis_size(axis)
    route = []
    for low in range(count):
        high = low | 1 << apart
        if high != low and high < count:
            route += [(low, high), (high, low)]
    return lax.ppermute(block, axis, route)


def lookup(substance_label, table):
    return jnp.where(
        substance_label == 0, table[0], jnp.where(substance_label == 1, table[1], table[2])
    )


def beside_all(source, axis_at, start_at):
    pieces = []
    for dim_at in range(3):
        length = source.shape[dim_at] - 2
        if dim_at == axis_at:
            pieces.append(slice(start_at, start_at + length))
        else:
            pieces.append(slice(1, 1 + length))
    return source[tuple(pieces)]


def advance(present_warmth, coupling_operator):
    centre = beside_all(present_warmth, 0, 1)
    middle = beside_all(coupling_operator, 0, 1)
    summed = jnp.zeros_like(centre)
    for axis_at in range(3):
        for start_at in (0, 2):
            coupling = 0.5 * (middle + beside_all(coupling_operator, axis_at, start_at))
            summed = summed + coupling * (beside_all(present_warmth, axis_at, start_at) - centre)
    return centre + summed


def per_device(
    thermal_state, substance_label, thermal_coefficients, optical_thickness, substance_colours
):
    sample_number, transverse_lines, marching_lines = thermal_state.shape
    coupling_operator = lookup(substance_label, thermal_coefficients)
    present_warmth = thermal_state
    conduct_wide = coupling_operator
    for substep in range(2):
        if substep == 0:
            stacked = jnp.stack([present_warmth, coupling_operator])
        else:
            stacked = present_warmth[None]
        x_widened = padded(stacked, (("sx", 2),), 1, True)
        widened = padded(x_widened, (("sy", 3), ("row", 1)), 1, False)
        if substep == 0:
            conduct_wide = widened[1]
        present_warmth = advance(widened[0], conduct_wide)
    glowing = jax.nn.sigmoid(present_warmth)
    opacity = (
        lookup(substance_label, optical_thickness)
        * glowing
        / (sample_number * lax.axis_size("row"))
    )
    through = jnp.cumprod(1.0 - opacity, axis=0)
    before = jnp.concatenate([jnp.ones_like(through[:1]), through[:-1]], axis=0)
    weight = before * opacity
    colours = [
        jnp.sum(weight * lookup(substance_label, substance_colours[:, channel]), axis=0)
        for channel in range(3)
    ]
    partial_image = jnp.stack(colours + [through[-1]])
    renderers = lax.axis_size("row")
    row_block = transverse_lines // renderers
    position = lax.axis_index("row")
    pieces = partial_image.reshape(4, renderers, row_block, marching_lines)
    for bit_number in range(renderers.bit_length() - 1):
        paired = pieces.reshape(4, pieces.shape[1] // 2, 2, row_block, marching_lines)
        bit_value = position >> bit_number & 1
        kept_half = lax.dynamic_index_in_dim(paired, bit_value, 2, keepdims=False)
        sent_half = lax.dynamic_index_in_dim(paired, 1 - bit_value, 2, keepdims=False)
        arrived = partner(sent_half, "row", bit_number)
        nearer = jnp.where(bit_value == 0, kept_half, arrived)
        farther = jnp.where(bit_value == 0, arrived, kept_half)
        pieces = jnp.concatenate(
            [nearer[:3] + nearer[3:] * farther[:3], nearer[3:] * farther[3:]], axis=0
        )
    blended = pieces.reshape(4, row_block, marching_lines)
    output_picture = jnp.concatenate([blended[:3], 1.0 - blended[3:]], axis=0)
    return (present_warmth, output_picture)


def solution(mesh):
    placed = (P("row", "sx", "sy"), P("row", "sx", "sy"), P(), P(), P())
    return jax.shard_map(
        per_device,
        mesh=mesh,
        in_specs=placed,
        out_specs=(P("row", "sx", "sy"), P(None, ("sx", "row"), "sy")),
        check_vma=False,
    )
```

profile of v0, /device:TPU:64, one launch (start us, length us, event | category | flops | bytes accessed | tf_op | source)
XLA Modules:
  0.0 125.4 jit_solution(4865847625222918080)
XLA Ops:
  0.6 0.0 copy-start.1
  0.6 1.4 %fusion.48 = (f32[1]{0:T(128)}, f32[1]{0:T(128)}, f32[1]{0:T(128)}) fusion(f32[3]{0:T(128)} %param.7), kind=kLoop, calls=%fused_computation.117 | loop fusion | bytes 24 | tf_op jit(solution)/shard_map/slice | solution.py:36
  2.0 4.3 %select_bitcast_fusion = (f32[1,32,64,128]{3,2,1,0:T(8,128)S(1)}, pred[32,64,128]{2,1,0:T(8,128)(4,1)}, pred[32,64,128]{2,1,0:T(8,128)(4,1)}) fusion(f32[]{:T(128)} %bitcast.3, f32[]{:T(128)} %bitcast.2, f32[]{:T(128)} %bitcast.1, s32[32,64,128]{2,1,0:T(8,128)} %param.6), kind=kLoop, calls=%fused_computation.62 | loop fusion | flops 1048576 | bytes 2621452 | tf_op jit(solution)/shard_map/stack | solution.py:71
  6.3 0.0 copy-done.1
  6.4 0.0 collective-permute-start
  6.4 2.9 %collective-permute-start.1 = (f32[2,32,1,128]{3,2,1,0:T(1,128)S(1)}, f32[2,32,1,128]{3,2,1,0:T(1,128)S(1)}, u32[]{:S(2)}, u32[]{:S(2)}) collective-permute-start(f32[2,32,1,128]{3,2,1,0:T(1,128)S(1)} %get-tuple-element.17), channel_id=1, source_target_pairs={{32,0},{64,32},{96,64},{128,96},{160,128},{192,160},{224,192},{0,2... | collective-permute-start | bytes 98312 | tf_op jit(solution)/shard_map/ppermute | solution.py:17
  9.3 1.6 %collective-permute-done = f32[2,32,1,128]{3,2,1,0:T(1,128)S(1)} collective-permute-done((f32[2,32,1,128]{3,2,1,0:T(1,128)S(1)}, f32[2,32,1,128]{3,2,1,0:T(1,128)S(1)}, u32[]{:S(2)}, u32[]{:S(2)}) %collective-permute-start) | collective-permute-done | bytes 32800 | tf_op jit(solution)/shard_map/ppermute | solution.py:15
  10.9 0.0 collective-permute-done.1
  10.9 0.3 pad_maximum_fusion.1
  11.3 2.2 %fusion.43 = (f32[2,32,66,1]{3,2,1,0:T(8,128)S(1)}, f32[2,32,66,1]{3,2,1,0:T(8,128)}) fusion(f32[2,32,66,128]{3,2,1,0:T(8,128)S(1)} %pad_maximum_fusion.1), kind=kLoop, calls=%fused_computation.112 | loop fusion | bytes 67584 | tf_op jit(solution)/shard_map/slice | solution.py:12
  13.4 2.4 %copy.8 = f32[2,32,66,1]{2,1,3,0:T(8,128)S(1)} copy(f32[2,32,66,1]{3,2,1,0:T(8,128)} %get-tuple-element.15) | data formatting | bytes 33792 | tf_op jit(solution)/shard_map/slice | solution.py:11
  15.9 3.3 %collective-permute-start.3 = (f32[2,32,66,1]{2,1,3,0:T(8,128)S(1)}, f32[2,32,66,1]{2,1,3,0:T(8,128)S(1)}, u32[]{:S(2)}, u32[]{:S(2)}) collective-permute-start(f32[2,32,66,1]{2,1,3,0:T(8,128)S(1)} %copy.8), channel_id=1, source_target_pairs={{8,0},{16,8},{24,16},{9,1},{17,9},{25,17},{10,2},{18,10},{26,18},{... | collective-permute-start | bytes 50696 | tf_op jit(solution)/shard_map/ppermute | solution.py:17
  19.2 1.4 %copy.7 = f32[2,32,66,1]{2,1,3,0:T(8,128)} copy(f32[2,32,66,1]{3,2,1,0:T(8,128)S(1)} %get-tuple-element.14) | data formatting | bytes 33792 | tf_op jit(solution)/shard_map/slice | solution.py:12
  20.6 5.0 %collective-permute-start.2 = (f32[2,32,66,1]{2,1,3,0:T(8,128)}, f32[2,32,66,1]{2,1,3,0:T(8,128)}, u32[]{:S(2)}, u32[]{:S(2)}) collective-permute-start(f32[2,32,66,1]{2,1,3,0:T(8,128)} %copy.7), channel_id=1, source_target_pairs={{0,8},{8,16},{16,24},{1,9},{9,17},{17,25},{2,10},{10,18},{18,26},{... | collective-permute-start | bytes 50696 | tf_op jit(solution)/shard_map/ppermute | solution.py:15
  25.7 0.0 collective-permute-done.3
  25.7 0.9 copy.10
  26.6 1.1 collective-permute-done.2
  27.7 3.0 %copy.9 = f32[2,32,66,1]{3,2,1,0:T(8,128)} copy(f32[2,32,66,1]{2,1,3,0:T(8,128)} %collective-permute-done.2) | data formatting | bytes 33792 | tf_op jit(solution)/shard_map/ppermute | solution.py:15
  30.7 1.3 %pad_maximum_fusion.8 = (f32[2,1,66,130]{3,2,1,0:T(8,128)S(1)}, f32[2,1,66,130]{3,2,1,0:T(8,128)S(1)}) fusion(f32[2,32,66,1]{3,2,1,0:T(8,128)S(1)} %copy.10, f32[2,32,66,1]{3,2,1,0:T(8,128)} %copy.9, f32[2,32,1,128]{3,2,1,0:T(1,128)S(1)} %collective-permute-done.1, f32[2,32,1,128]{3,2,1,0:T(1,128)S(1)} %collective-permute-done, ...), kind=kLoop, calls=%fused_computation.71 | loop fusion | flops 171600 | bytes 2333760 | tf_op jit(solution)/shard_map/slice | solution.py:12
  32.0 3.5 %collective-permute-start.4 = (f32[2,1,66,130]{3,2,1,0:T(8,128)S(1)}, f32[2,1,66,130]{3,2,1,0:T(8,128)S(1)}, u32[]{:S(2)}, u32[]{:S(2)}) collective-permute-start(f32[2,1,66,130]{3,2,1,0:T(8,128)S(1)} %get-tuple-element.8), channel_id=1, source_target_pairs={{0,1},{1,2},{2,3},{3,4},{4,5},{5,6},{6,7},{8,9},{9,10},{10,11},{11... | collective-permute-start | bytes 205928 | tf_op jit(solution)/shard_map/ppermute | solution.py:15
  35.5 1.3 %collective-permute-start.5 = (f32[2,1,66,130]{3,2,1,0:T(8,128)S(1)}, f32[2,1,66,130]{3,2,1,0:T(8,128)S(1)}, u32[]{:S(2)}, u32[]{:S(2)}) collective-permute-start(f32[2,1,66,130]{3,2,1,0:T(8,128)S(1)} %get-tuple-element.9), channel_id=1, source_target_pairs={{1,0},{2,1},{3,2},{4,3},{5,4},{6,5},{7,6},{9,8},{10,9},{11,10},{12... | collective-permute-start | bytes 205928 | tf_op jit(solution)/shard_map/ppermute | solution.py:17
  36.8 1.3 %collective-permute-done.4 = f32[2,1,66,130]{3,2,1,0:T(8,128)S(1)} collective-permute-done((f32[2,1,66,130]{3,2,1,0:T(8,128)S(1)}, f32[2,1,66,130]{3,2,1,0:T(8,128)S(1)}, u32[]{:S(2)}, u32[]{:S(2)}) %collective-permute-start.4) | collective-permute-done | bytes 68672 | tf_op jit(solution)/shard_map/ppermute | solution.py:15
  38.1 5.1 %collective-permute-done.5 = f32[2,1,66,130]{3,2,1,0:T(8,128)S(1)} collective-permute-done((f32[2,1,66,130]{3,2,1,0:T(8,128)S(1)}, f32[2,1,66,130]{3,2,1,0:T(8,128)S(1)}, u32[]{:S(2)}, u32[]{:S(2)}) %collective-permute-start.5) | collective-permute-done | bytes 68672 | tf_op jit(solution)/shard_map/ppermute | solution.py:17
  43.2 0.0 copy-done
  43.2 4.4 %pad_maximum_fusion = f32[2,34,66,130]{3,2,1,0:T(8,128)S(1)} fusion(f32[2,1,66,130]{3,2,1,0:T(8,128)S(1)} %collective-permute-done.5, f32[2,32,66,1]{3,2,1,0:T(8,128)S(1)} %copy.10, f32[2,32,1,128]{3,2,1,0:T(1,128)S(1)} %collective-permute-done.1, f32[1,32,64,128]{3,2,1,0:T(8,128)S(1)} %get-tuple-element.5, f32[1,32,64,128]{3,2,1,0:T(8,128)S(1)} %bitcast.54, ...), kind=kLoop, calls=%fused_computation | loop fusion | flops 4084080 | bytes 4667520 | tf_op jit(solution)/shard_map/concatenate | solution.py:13
  47.6 0.3 slice_bitcast_fusion
  48.0 3.8 %fusion.15 = f32[1,32,64,128]{3,2,1,0:T(8,128)S(1)} fusion(f32[34,66,130]{2,1,0:T(8,128)S(1)} %get-tuple-element.11, f32[34,66,130]{2,1,0:T(8,128)S(1)} %get-tuple-element.10), kind=kLoop, calls=%fused_computation.28 | loop fusion | flops 7864320 | bytes 15728640 | tf_op jit(solution)/shard_map/broadcast_in_dim | solution.py:73
  51.8 0.0 collective-permute-start.6
  51.9 2.9 %collective-permute-start.7 = (f32[1,32,1,128]{3,2,1,0:T(1,128)S(1)}, f32[1,32,1,128]{3,2,1,0:T(1,128)S(1)}, u32[]{:S(2)}, u32[]{:S(2)}) collective-permute-start(f32[1,32,1,128]{3,2,1,0:T(1,128)S(1)} %get-tuple-element.21), channel_id=1, source_target_pairs={{32,0},{64,32},{96,64},{128,96},{160,128},{192,160},{224,192},{0,2... | collective-permute-start | bytes 49160 | tf_op jit(solution)/shard_map/ppermute | solution.py:17
  54.8 1.4 %collective-permute-done.6 = f32[1,32,1,128]{3,2,1,0:T(1,128)S(1)} collective-permute-done((f32[1,32,1,128]{3,2,1,0:T(1,128)S(1)}, f32[1,32,1,128]{3,2,1,0:T(1,128)S(1)}, u32[]{:S(2)}, u32[]{:S(2)}) %collective-permute-start.6) | collective-permute-done | bytes 16416 | tf_op jit(solution)/shard_map/ppermute | solution.py:15
  56.2 0.0 collective-permute-done.7
  56.2 0.6 copy-done.6
  56.8 0.6 copy-done.7
  57.4 0.1 pad_maximum_fusion.2
  57.5 1.8 %fusion.44 = (f32[1,32,66,1]{3,2,1,0:T(8,128)}, f32[1,32,66,1]{3,2,1,0:T(8,128)}) fusion(f32[1,32,66,128]{3,2,1,0:T(8,128)S(1)} %pad_maximum_fusion.2), kind=kLoop, calls=%fused_computation.113 | loop fusion | bytes 33792 | tf_op jit(solution)/shard_map/slice | solution.py:12
  59.3 2.3 %copy.11 = f32[1,32,66,1]{2,1,3,0:T(8,128)} copy(f32[1,32,66,1]{3,2,1,0:T(8,128)} %get-tuple-element.18) | data formatting | bytes 16896 | tf_op jit(solution)/shard_map/slice | solution.py:12
  61.7 6.1 %collective-permute-start.8 = (f32[1,32,66,1]{2,1,3,0:T(8,128)}, f32[1,32,66,1]{2,1,3,0:T(8,128)}, u32[]{:S(2)}, u32[]{:S(2)}) collective-permute-start(f32[1,32,66,1]{2,1,3,0:T(8,128)} %copy.11), channel_id=1, source_target_pairs={{0,8},{8,16},{16,24},{1,9},{9,17},{17,25},{2,10},{10,18},{18,26},{... | collective-permute-start | bytes 25352 | tf_op jit(solution)/shard_map/ppermute | solution.py:15
  67.8 2.3 %copy.12 = f32[1,32,66,1]{2,1,3,0:T(8,128)} copy(f32[1,32,66,1]{3,2,1,0:T(8,128)} %get-tuple-element.19) | data formatting | bytes 16896 | tf_op jit(solution)/shard_map/slice | solution.py:11
  70.1 1.9 %collective-permute-start.9 = (f32[1,32,66,1]{2,1,3,0:T(8,128)}, f32[1,32,66,1]{2,1,3,0:T(8,128)}, u32[]{:S(2)}, u32[]{:S(2)}) collective-permute-start(f32[1,32,66,1]{2,1,3,0:T(8,128)} %copy.12), channel_id=1, source_target_pairs={{8,0},{16,8},{24,16},{9,1},{17,9},{25,17},{10,2},{18,10},{26,18},{... | collective-permute-start | bytes 25352 | tf_op jit(solution)/shard_map/ppermute | solution.py:17
  72.0 1.7 %fusion.46 = (f32[1,1]{1,0:T(1,128)}, f32[1,1]{1,0:T(1,128)}, f32[1,1]{1,0:T(1,128)}, f32[1,1]{1,0:T(1,128)}, f32[1,1]{1,0:T(1,128)}, /*index=5*/f32[1,1]{1,0:T(...) fusion(f32[3,3]{1,0:T(4,128)} %param.9), kind=kLoop, calls=%fused_computation.115 | loop fusion | bytes 72 | tf_op jit(solution)/shard_map/slice | solution.py:36
  73.7 0.0 collective-permute-done.8
  73.7 2.2 %copy.13 = f32[1,32,66,1]{3,2,1,0:T(8,128)} copy(f32[1,32,66,1]{2,1,3,0:T(8,128)} %collective-permute-done.8) | data formatting | bytes 16896 | tf_op jit(solution)/shard_map/ppermute | solution.py:15
  75.9 2.2 %collective-permute-done.9 = f32[1,32,66,1]{2,1,3,0:T(8,128)} collective-permute-done((f32[1,32,66,1]{2,1,3,0:T(8,128)}, f32[1,32,66,1]{2,1,3,0:T(8,128)}, u32[]{:S(2)}, u32[]{:S(2)}) %collective-permute-start.9) | collective-permute-done | bytes 8480 | tf_op jit(solution)/shard_map/ppermute | solution.py:17
  78.2 2.2 %copy.14 = f32[1,32,66,1]{3,2,1,0:T(8,128)} copy(f32[1,32,66,1]{2,1,3,0:T(8,128)} %collective-permute-done.9) | data formatting | bytes 16896 | tf_op jit(solution)/shard_map/ppermute | solution.py:17
  80.4 1.6 %pad_maximum_fusion.14 = (f32[1,1,66,130]{3,2,1,0:T(8,128)}, f32[1,1,66,130]{3,2,1,0:T(8,128)}) fusion(f32[1,32,66,1]{3,2,1,0:T(8,128)} %copy.14, f32[1,32,66,1]{3,2,1,0:T(8,128)} %copy.13, f32[1,32,1,128]{3,2,1,0:T(1,128)} %copy-done.7, f32[1,32,64,128]{3,2,1,0:T(8,128)S(1)} %fusion.15, f32[1,32,1,128]{3,2,1,0:T(1,128)} %copy-done.6), kind=kLoop, calls=%fused_computation.77 | loop fusion | flops 68640 | bytes 1166880 | tf_op jit(solution)/shard_map/slice | solution.py:12
  82.0 4.7 %collective-permute-start.10 = (f32[1,1,66,130]{3,2,1,0:T(8,128)}, f32[1,1,66,130]{3,2,1,0:T(8,128)}, u32[]{:S(2)}, u32[]{:S(2)}) collective-permute-start(f32[1,1,66,130]{3,2,1,0:T(8,128)} %get-tuple-element.12), channel_id=1, source_target_pairs={{0,1},{1,2},{2,3},{3,4},{4,5},{5,6},{6,7},{8,9},{9,10},{10,11},{11... | collective-permute-start | bytes 102968 | tf_op jit(solution)/shard_map/ppermute | solution.py:15
  86.7 1.5 %collective-permute-start.11 = (f32[1,1,66,130]{3,2,1,0:T(8,128)}, f32[1,1,66,130]{3,2,1,0:T(8,128)}, u32[]{:S(2)}, u32[]{:S(2)}) collective-permute-start(f32[1,1,66,130]{3,2,1,0:T(8,128)} %get-tuple-element.13), channel_id=1, source_target_pairs={{1,0},{2,1},{3,2},{4,3},{5,4},{6,5},{7,6},{9,8},{10,9},{11,10},{12... | collective-permute-start | bytes 102968 | tf_op jit(solution)/shard_map/ppermute | solution.py:17
  88.2 0.7 fusion.47
  88.9 0.0 collective-permute-done.10
  88.9 4.4 %collective-permute-done.11 = f32[1,1,66,130]{3,2,1,0:T(8,128)} collective-permute-done((f32[1,1,66,130]{3,2,1,0:T(8,128)}, f32[1,1,66,130]{3,2,1,0:T(8,128)}, u32[]{:S(2)}, u32[]{:S(2)}) %collective-permute-start.11) | collective-permute-done | bytes 34352 | tf_op jit(solution)/shard_map/ppermute | solution.py:17
  93.3 2.8 %maximum_bitcast_fusion = f32[34,66,130]{2,1,0:T(8,128)S(1)} fusion(f32[1,1,66,130]{3,2,1,0:T(8,128)} %collective-permute-done.11, f32[1,32,66,1]{3,2,1,0:T(8,128)} %copy.14, f32[1,32,1,128]{3,2,1,0:T(1,128)} %copy-done.7, f32[1,32,64,128]{3,2,1,0:T(8,128)S(1)} %fusion.15, f32[1,32,1,128]{3,2,1,0:T(1,128)} %copy-done.6, f32[1,32,66,1]{3,2,1,0:T(8,128)} %copy.13, ...), kind=kLoop, calls=%fused_computation.3 | loop fusion | flops 1750320 | bytes 2333760 | tf_op jit(solution)/shard_map/squeeze | solution.py:78
  96.1 0.0 copy-start.4
  96.1 3.8 %fusion.2 = f32[32,64,128]{2,1,0:T(8,128)S(1)} fusion(f32[34,66,130]{2,1,0:T(8,128)S(1)} %maximum_bitcast_fusion, f32[34,66,130]{2,1,0:T(8,128)S(1)} %get-tuple-element.10), kind=kLoop, calls=%fused_computation.9 | loop fusion | flops 7864320 | bytes 15728640 | tf_op jit(solution)/shard_map/add | solution.py:59
  99.9 0.0 copy-start.3
  100.0 2.4 %fusion.31 = f32[32,64,128]{2,1,0:T(8,128)S(1)} fusion(f32[32,64,128]{2,1,0:T(8,128)S(1)} %fusion.2, pred[32,64,128]{2,1,0:T(8,128)(4,1)S(1)} %copy-done.5, pred[32,64,128]{2,1,0:T(8,128)(4,1)S(1)} %copy-done.4, f32[]{:T(128)} %bitcast.11, f32[]{:T(128)} %bitcast.10, f32[]{:T(128)} %bitcast.9), kind=kOutput, calls=%fused_computation.59 | output fusion | flops 10223616 | bytes 2621452 | tf_op jit(solution)/shard_map/jit(cumprod)/reduce_window | solution.py:85
  102.4 0.1 slice.323
  102.5 8.3 %multiply_reduce_fusion.2 = (f32[64,128]{1,0:T(8,128)S(1)}, f32[64,128]{1,0:T(8,128)S(1)}, f32[64,128]{1,0:T(8,128)S(1)}) fusion(pred[32,64,128]{2,1,0:T(8,128)(4,1)S(1)} %copy-done.5, pred[32,64,128]{2,1,0:T(8,128)(4,1)S(1)} %copy-done.4, f32[]{:T(128)} %bitcast.14, f32[]{:T(128)} %bitcast.13, f32[]{:T(128)} %bitcast.12, f32[31,64,128]{2,1,0:T(8,128)S(1)} %slice.323, ...), kind=kLoop, calls=%fused_computation.57 | loop fusion | flops 5218304 | bytes 2687024 | tf_op jit(solution)/shard_map/reduce_sum | solution.py:89
  110.9 1.2 collective-permute-start.12
  112.1 3.2 %collective-permute-done.12 = f32[4,4,8,128]{3,2,1,0:T(8,128)S(1)} collective-permute-done((f32[4,4,8,128]{3,2,1,0:T(8,128)S(1)}, f32[4,4,8,128]{3,2,1,0:T(8,128)S(1)}, u32[]{:S(2)}, u32[]{:S(2)}) %collective-permute-start.12) | collective-permute-done | bytes 65568 | tf_op jit(solution)/shard_map/ppermute | solution.py:31
  115.4 1.0 collective-permute-start.13
  116.3 3.0 %collective-permute-done.13 = f32[4,2,8,128]{3,2,1,0:T(8,128)S(1)} collective-permute-done((f32[4,2,8,128]{3,2,1,0:T(8,128)S(1)}, f32[4,2,8,128]{3,2,1,0:T(8,128)S(1)}, u32[]{:S(2)}, u32[]{:S(2)}) %collective-permute-start.13) | collective-permute-done | bytes 32800 | tf_op jit(solution)/shard_map/ppermute | solution.py:31
  119.4 2.2 %collective-permute-start.14 = (f32[4,1,8,128]{3,2,1,0:T(8,128)S(1)}, f32[4,1,8,128]{3,2,1,0:T(8,128)S(1)}, u32[]{:S(2)}, u32[]{:S(2)}) collective-permute-start(f32[4,1,8,128]{3,2,1,0:T(8,128)S(1)} %fusion.36), channel_id=1, source_target_pairs={{0,4},{4,0},{1,5},{5,1},{2,6},{6,2},{3,7},{7,3},{8,12},{12,8},{9,1... | collective-permute-start | bytes 49160 | tf_op jit(solution)/shard_map/ppermute | solution.py:31
  121.6 3.1 %collective-permute-done.14 = f32[4,1,8,128]{3,2,1,0:T(8,128)S(1)} collective-permute-done((f32[4,1,8,128]{3,2,1,0:T(8,128)S(1)}, f32[4,1,8,128]{3,2,1,0:T(8,128)S(1)}, u32[]{:S(2)}, u32[]{:S(2)}) %collective-permute-start.14) | collective-permute-done | bytes 16416 | tf_op jit(solution)/shard_map/ppermute | solution.py:31
  124.8 0.6 pad_maximum_fusion.18
  (28 shorter events, 0.2 us)
Async XLA Ops:
  0.6 5.7 %copy-start.1 = (f32[32,64,128]{2,1,0:T(8,128)S(1)}, f32[32,64,128]{2,1,0:T(8,128)}, u32[]{:S(2)}) copy-start(f32[32,64,128]{2,1,0:T(8,128)} %param.5) | copy-start | bytes 3145732
  6.4 4.6 %collective-permute-start = (f32[2,32,1,128]{3,2,1,0:T(1,128)S(1)}, f32[2,32,1,128]{3,2,1,0:T(1,128)S(1)}, u32[]{:S(2)}, u32[]{:S(2)}) collective-permute-start(f32[2,32,1,128]{3,2,1,0:T(1,128)S(1)} %get-tuple-element.16), channel_id=1, source_target_pairs={{0,32},{32,64},{64,96},{96,128},{128,160},{160,192},{192,224},{224... | collective-permute-start | bytes 98312 | tf_op jit(solution)/shard_map/ppermute | solution.py:15
  6.4 4.5 %collective-permute-start.1 = (f32[2,32,1,128]{3,2,1,0:T(1,128)S(1)}, f32[2,32,1,128]{3,2,1,0:T(1,128)S(1)}, u32[]{:S(2)}, u32[]{:S(2)}) collective-permute-start(f32[2,32,1,128]{3,2,1,0:T(1,128)S(1)} %get-tuple-element.17), channel_id=1, source_target_pairs={{32,0},{64,32},{96,64},{128,96},{160,128},{192,160},{224,192},{0,2... | collective-permute-start | bytes 98312 | tf_op jit(solution)/shard_map/ppermute | solution.py:17
  15.9 9.8 %collective-permute-start.3 = (f32[2,32,66,1]{2,1,3,0:T(8,128)S(1)}, f32[2,32,66,1]{2,1,3,0:T(8,128)S(1)}, u32[]{:S(2)}, u32[]{:S(2)}) collective-permute-start(f32[2,32,66,1]{2,1,3,0:T(8,128)S(1)} %copy.8), channel_id=1, source_target_pairs={{8,0},{16,8},{24,16},{9,1},{17,9},{25,17},{10,2},{18,10},{26,18},{... | collective-permute-start | bytes 50696 | tf_op jit(solution)/shard_map/ppermute | solution.py:17
  20.6 7.0 %collective-permute-start.2 = (f32[2,32,66,1]{2,1,3,0:T(8,128)}, f32[2,32,66,1]{2,1,3,0:T(8,128)}, u32[]{:S(2)}, u32[]{:S(2)}) collective-permute-start(f32[2,32,66,1]{2,1,3,0:T(8,128)} %copy.7), channel_id=1, source_target_pairs={{0,8},{8,16},{16,24},{1,9},{9,17},{17,25},{2,10},{10,18},{18,26},{... | collective-permute-start | bytes 50696 | tf_op jit(solution)/shard_map/ppermute | solution.py:15
  30.7 12.5 %copy-start = (f32[2,32,66,1]{3,2,1,0:T(8,128)S(1)}, f32[2,32,66,1]{3,2,1,0:T(8,128)}, u32[]{:S(2)}) copy-start(f32[2,32,66,1]{3,2,1,0:T(8,128)} %copy.9) | copy-start | bytes 50692
  30.7 12.5 %copy-start.2 = (f32[32,64,128]{2,1,0:T(8,128)S(1)}, f32[32,64,128]{2,1,0:T(8,128)}, u32[]{:S(2)}) copy-start(f32[32,64,128]{2,1,0:T(8,128)} %param.5) | copy-start | bytes 3145732
  32.0 6.2 %collective-permute-start.4 = (f32[2,1,66,130]{3,2,1,0:T(8,128)S(1)}, f32[2,1,66,130]{3,2,1,0:T(8,128)S(1)}, u32[]{:S(2)}, u32[]{:S(2)}) collective-permute-start(f32[2,1,66,130]{3,2,1,0:T(8,128)S(1)} %get-tuple-element.8), channel_id=1, source_target_pairs={{0,1},{1,2},{2,3},{3,4},{4,5},{5,6},{6,7},{8,9},{9,10},{10,11},{11... | collective-permute-start | bytes 205928 | tf_op jit(solution)/shard_map/ppermute | solution.py:15
  35.5 7.7 %collective-permute-start.5 = (f32[2,1,66,130]{3,2,1,0:T(8,128)S(1)}, f32[2,1,66,130]{3,2,1,0:T(8,128)S(1)}, u32[]{:S(2)}, u32[]{:S(2)}) collective-permute-start(f32[2,1,66,130]{3,2,1,0:T(8,128)S(1)} %get-tuple-element.9), channel_id=1, source_target_pairs={{1,0},{2,1},{3,2},{4,3},{5,4},{6,5},{7,6},{9,8},{10,9},{11,10},{12... | collective-permute-start | bytes 205928 | tf_op jit(solution)/shard_map/ppermute | solution.py:17
  51.8 4.4 %collective-permute-start.6 = (f32[1,32,1,128]{3,2,1,0:T(1,128)S(1)}, f32[1,32,1,128]{3,2,1,0:T(1,128)S(1)}, u32[]{:S(2)}, u32[]{:S(2)}) collective-permute-start(f32[1,32,1,128]{3,2,1,0:T(1,128)S(1)} %get-tuple-element.20), channel_id=1, source_target_pairs={{0,32},{32,64},{64,96},{96,128},{128,160},{160,192},{192,224},{224... | collective-permute-start | bytes 49160 | tf_op jit(solution)/shard_map/ppermute | solution.py:15
  51.9 4.4 %collective-permute-start.7 = (f32[1,32,1,128]{3,2,1,0:T(1,128)S(1)}, f32[1,32,1,128]{3,2,1,0:T(1,128)S(1)}, u32[]{:S(2)}, u32[]{:S(2)}) collective-permute-start(f32[1,32,1,128]{3,2,1,0:T(1,128)S(1)} %get-tuple-element.21), channel_id=1, source_target_pairs={{32,0},{64,32},{96,64},{128,96},{160,128},{192,160},{224,192},{0,2... | collective-permute-start | bytes 49160 | tf_op jit(solution)/shard_map/ppermute | solution.py:17
  56.2 0.6 copy-start.6
  56.8 0.6 copy-start.7
  61.7 12.1 %collective-permute-start.8 = (f32[1,32,66,1]{2,1,3,0:T(8,128)}, f32[1,32,66,1]{2,1,3,0:T(8,128)}, u32[]{:S(2)}, u32[]{:S(2)}) collective-permute-start(f32[1,32,66,1]{2,1,3,0:T(8,128)} %copy.11), channel_id=1, source_target_pairs={{0,8},{8,16},{16,24},{1,9},{9,17},{17,25},{2,10},{10,18},{18,26},{... | collective-permute-start | bytes 25352 | tf_op jit(solution)/shard_map/ppermute | solution.py:15
  70.1 8.1 %collective-permute-start.9 = (f32[1,32,66,1]{2,1,3,0:T(8,128)}, f32[1,32,66,1]{2,1,3,0:T(8,128)}, u32[]{:S(2)}, u32[]{:S(2)}) collective-permute-start(f32[1,32,66,1]{2,1,3,0:T(8,128)} %copy.12), channel_id=1, source_target_pairs={{8,0},{16,8},{24,16},{9,1},{17,9},{25,17},{10,2},{18,10},{26,18},{... | collective-permute-start | bytes 25352 | tf_op jit(solution)/shard_map/ppermute | solution.py:17
  80.4 7.8 %copy-start.8 = (f32[3]{0:T(128)S(1)}, f32[3]{0:T(128)}, u32[]{:S(2)}) copy-start(f32[3]{0:T(128)} %param.8) | copy-start | bytes 40
  82.0 6.9 %collective-permute-start.10 = (f32[1,1,66,130]{3,2,1,0:T(8,128)}, f32[1,1,66,130]{3,2,1,0:T(8,128)}, u32[]{:S(2)}, u32[]{:S(2)}) collective-permute-start(f32[1,1,66,130]{3,2,1,0:T(8,128)} %get-tuple-element.12), channel_id=1, source_target_pairs={{0,1},{1,2},{2,3},{3,4},{4,5},{5,6},{6,7},{8,9},{9,10},{10,11},{11... | collective-permute-start | bytes 102968 | tf_op jit(solution)/shard_map/ppermute | solution.py:15
  86.7 6.6 %collective-permute-start.11 = (f32[1,1,66,130]{3,2,1,0:T(8,128)}, f32[1,1,66,130]{3,2,1,0:T(8,128)}, u32[]{:S(2)}, u32[]{:S(2)}) collective-permute-start(f32[1,1,66,130]{3,2,1,0:T(8,128)} %get-tuple-element.13), channel_id=1, source_target_pairs={{1,0},{2,1},{3,2},{4,3},{5,4},{6,5},{7,6},{9,8},{10,9},{11,10},{12... | collective-permute-start | bytes 102968 | tf_op jit(solution)/shard_map/ppermute | solution.py:17
  96.1 3.9 %copy-start.4 = (pred[32,64,128]{2,1,0:T(8,128)(4,1)S(1)}, pred[32,64,128]{2,1,0:T(8,128)(4,1)}, u32[]{:S(2)}) copy-start(pred[32,64,128]{2,1,0:T(8,128)(4,1)} %get-tuple-element.6) | copy-start | bytes 786436
  96.1 3.9 %copy-start.5 = (pred[32,64,128]{2,1,0:T(8,128)(4,1)S(1)}, pred[32,64,128]{2,1,0:T(8,128)(4,1)}, u32[]{:S(2)}) copy-start(pred[32,64,128]{2,1,0:T(8,128)(4,1)} %get-tuple-element.7) | copy-start | bytes 786436
  99.9 10.9 %copy-start.3 = (f32[32,64,128]{2,1,0:T(8,128)}, f32[32,64,128]{2,1,0:T(8,128)S(1)}, u32[]{:S(2)}) copy-start(f32[32,64,128]{2,1,0:T(8,128)S(1)} %fusion.2) | copy-start | bytes 3145732
  110.9 4.4 %collective-permute-start.12 = (f32[4,4,8,128]{3,2,1,0:T(8,128)S(1)}, f32[4,4,8,128]{3,2,1,0:T(8,128)S(1)}, u32[]{:S(2)}, u32[]{:S(2)}) collective-permute-start(f32[4,4,8,128]{3,2,1,0:T(8,128)S(1)} %dynamic-slice_bitcast_fusion), channel_id=1, source_target_pairs={{0,1},{1,0},{2,3},{3,2},{4,5},{5,4},{6,7},{7,6},{8,9},{9,8},{10,11... | collective-permute-start | bytes 196616 | tf_op jit(solution)/shard_map/ppermute | solution.py:31
  115.4 4.0 %collective-permute-start.13 = (f32[4,2,8,128]{3,2,1,0:T(8,128)S(1)}, f32[4,2,8,128]{3,2,1,0:T(8,128)S(1)}, u32[]{:S(2)}, u32[]{:S(2)}) collective-permute-start(f32[4,2,8,128]{3,2,1,0:T(8,128)S(1)} %dynamic-slice_bitcast_fusion.1), channel_id=1, source_target_pairs={{0,2},{2,0},{1,3},{3,1},{4,6},{6,4},{5,7},{7,5},{8,10},{10,8},{9,1... | collective-permute-start | bytes 98312 | tf_op jit(solution)/shard_map/ppermute | solution.py:31
  119.4 5.3 %collective-permute-start.14 = (f32[4,1,8,128]{3,2,1,0:T(8,128)S(1)}, f32[4,1,8,128]{3,2,1,0:T(8,128)S(1)}, u32[]{:S(2)}, u32[]{:S(2)}) collective-permute-start(f32[4,1,8,128]{3,2,1,0:T(8,128)S(1)} %fusion.36), channel_id=1, source_target_pairs={{0,4},{4,0},{1,5},{5,1},{2,6},{6,2},{3,7},{7,3},{8,12},{12,8},{9,1... | collective-permute-start | bytes 49160 | tf_op jit(solution)/shard_map/ppermute | solution.py:31
where the time goes:
time: 126 us; the launch traced here: 125 us
  starting transfers between devices  37.6 us (30%)
  other arithmetic  34.1 us (27%)
  waiting for transfers between devices  26.5 us (21%)
  local copies, waits for them, and re-layouts  26.2 us (21%)
    ppermute x6, starting transfers between devices, padded(): lax.ppermute(tail, axis, [(i, (i + 1) % count) for i in range(ends)])  19.4 us
    ppermute x6, starting transfers between devices, padded(): lax.ppermute(head, axis, [((i + 1) % count, i) for i in range(ends)])  13.9 us
    ppermute x6, waiting for transfers between devices, padded(): lax.ppermute(head, axis, [((i + 1) % count, i) for i in range(ends)])  11.8 us
    ppermute x3, waiting for transfers between devices, partner(): return lax.ppermute(block, axis, route)  9.36 us
    reduce_sum x1, other arithmetic, per_device(): jnp.sum(weight * lookup(substance_label, substance_colours[:, channel]),...  8.34 us
    slice x5, local copies, waits for them, and re-layouts, padded(): lax.slice_in_dim(cells, cells.shape[dim] - width, cells.shape[dim], axis=...  7.74 us
    ppermute x6, waiting for transfers between devices, padded(): lax.ppermute(tail, axis, [(i, (i + 1) % count) for i in range(ends)])  5.43 us
    ppermute x2, local copies, waits for them, and re-layouts, padded(): lax.ppermute(tail, axis, [(i, (i + 1) % count) for i in range(ends)])  5.23 us
  transfers between devices with their start and end apart: 15, of which 10 were waited for; matrix products, arithmetic and copies ran while one was open for 7% of the time, Pallas kernels for 0%

commit v1 on v0

v1 whole, which is shorter than its diff:
```python
import functools

import jax
import jax.numpy as jnp
from jax import lax
from jax.experimental import pallas as pl
from jax.experimental.pallas import tpu as pltpu
from jax.sharding import PartitionSpec as P

MESH = pl.DeviceIdType.MESH
SUB, LANES = 8, 128


def kernel(
    sizes,
    t_hbm, lab_hbm, coef_hbm, thick_hbm, tint_hbm,
    out_hbm, pic_ref,
    u, d, h, f, lab, xs, xr, xs2, xr2, ys, yr, ys2, yr2, mid, ib, rb,
    coef, thick, tint, lsem, ssem, rsem, asem, bsem,
):
    n_sx, n_sy, n_row = sizes
    depth, wide = lab.shape[0], lab.shape[1]
    blocks = wide // SUB
    per_group = LANES // depth
    groups = blocks // per_group
    chunks = depth // SUB
    last = depth
    me, my_sx, my_sy = lax.axis_index("row"), lax.axis_index("sx"), lax.axis_index("sy")
    has_prev, has_next = me > 0, me < n_row - 1
    has_left, has_right = my_sy > 0, my_sy < n_sy - 1

    load_t = pltpu.make_async_copy(t_hbm, u.at[pl.ds(1, depth)], lsem.at[0])
    load_l = pltpu.make_async_copy(lab_hbm, lab, lsem.at[1])
    load_c = pltpu.make_async_copy(coef_hbm, coef, lsem.at[2])
    load_k = pltpu.make_async_copy(thick_hbm, thick, lsem.at[3])
    load_p = pltpu.make_async_copy(tint_hbm, tint, lsem.at[4])
    load_c.start()
    load_l.start()
    load_t.start()
    load_k.start()
    load_p.start()

    barrier = pltpu.get_barrier_semaphore()
    for o in range(1, n_row):
        pl.semaphore_signal(barrier, inc=1, device_id={"row": lax.rem(me + o, n_row)}, device_id_type=MESH)
    sx_next = lax.rem(my_sx + 1, n_sx)
    sx_prev = lax.rem(my_sx + n_sx - 1, n_sx)
    pl.semaphore_signal(barrier, inc=1, device_id={"sx": sx_next}, device_id_type=MESH)
    pl.semaphore_signal(barrier, inc=1, device_id={"sx": sx_prev}, device_id_type=MESH)

    @pl.when(has_left)
    def _():
        pl.semaphore_signal(barrier, inc=1, device_id={"sy": my_sy - 1}, device_id_type=MESH)

    @pl.when(has_right)
    def _():
        pl.semaphore_signal(barrier, inc=1, device_id={"sy": my_sy + 1}, device_id_type=MESH)

    lane = lax.broadcasted_iota(jnp.int32, (SUB, LANES), 1)
    sub = lax.broadcasted_iota(jnp.int32, (SUB, LANES), 0)
    lane_after = lax.rem(lane + 1, LANES)
    at_ends = (lane == 0) | (lane == LANES - 1)
    is_even = lax.rem(lane, 2) == 0
    zero = jnp.zeros((SUB, LANES), jnp.float32)

    @pl.when(jnp.logical_not(has_prev))
    def _():
        for a in (u, d, h):
            a[0] = jnp.zeros((wide, LANES), jnp.float32)

    @pl.when(jnp.logical_not(has_next))
    def _():
        for a in (u, d, h):
            a[depth + 1] = jnp.zeros((wide, LANES), jnp.float32)

    @pl.when(jnp.logical_not(has_left))
    def _():
        yr[0] = jnp.zeros(yr.shape[1:], jnp.float32)
        yr2[0] = jnp.zeros(yr2.shape[1:], jnp.float32)

    @pl.when(jnp.logical_not(has_right))
    def _():
        yr[1] = jnp.zeros(yr.shape[1:], jnp.float32)
        yr2[1] = jnp.zeros(yr2.shape[1:], jnp.float32)

    def rows(xb):
        return pl.ds(SUB * xb, SUB)

    def spot(z0, xb):
        return depth * (xb % per_group) + z0

    load_c.wait()
    c0, c1, c2 = 0.5 * coef[0], 0.5 * coef[1], 0.5 * coef[2]
    load_l.wait()
    load_t.wait()

    def put(acc, v, m, xb):
        left, right = acc
        r = pltpu.roll(v, m, 1)
        g = xb // per_group
        left[g] = jnp.where(lane == m, r, left[g])
        right[g] = jnp.where(lane_after == m, r, right[g])

    def pack_first(z0, carry):
        lu, ru, ld, rd = [list(c) for c in carry]
        for xb in range(blocks):
            v = u[z0 + 1, rows(xb), :]
            lb = lab[z0, rows(xb), :]
            dv = jnp.where(lb == 0, c0, jnp.where(lb == 1, c1, c2))
            d[z0 + 1, rows(xb), :] = dv
            m = spot(z0, xb)
            put((lu, ru), v, m, xb)
            put((ld, rd), dv, m, xb)
        return tuple(tuple(c) for c in (lu, ru, ld, rd))

    empty = (zero,) * groups
    lu, ru, ld, rd = lax.fori_loop(0, depth, pack_first, (empty,) * 4)
    for g in range(groups):
        at = pl.ds(SUB * g, SUB)
        ys[0, 0, at, :] = lu[g]
        ys[0, 1, at, :] = ld[g]
        ys[1, 0, at, :] = pltpu.roll(ru[g], 1, 1)
        ys[1, 1, at, :] = pltpu.roll(rd[g], 1, 1)

    def edge(ref, first, k, side):
        row = (wide - 1) * side
        flat = ref.reshape(ref.shape[0] * wide, LANES)
        return flat, pl.ds((first + SUB * k) * wide + row, SUB, stride=wide)

    for side in (0, 1):
        for k in range(chunks):
            for i, a in enumerate((u, d)):
                flat, at = edge(a, 1, k, side)
                xs[side, i, pl.ds(SUB * k, SUB), :] = flat[at, :]

    def remote(src, dst, s, where):
        return pltpu.make_async_remote_copy(
            src_ref=src, dst_ref=dst, send_sem=ssem.at[s], recv_sem=rsem.at[s],
            device_id=where, device_id_type=MESH,
        )

    to_next, to_prev = {"row": me + 1}, {"row": me - 1}
    to_right, to_left = {"sy": my_sy + 1}, {"sy": my_sy - 1}
    to_up, to_down = {"sx": sx_next}, {"sx": sx_prev}
    z_first = [
        (remote(u.at[last], u.at[0], 0, to_next), has_next, has_prev),
        (remote(d.at[last], d.at[0], 1, to_next), has_next, has_prev),
        (remote(u.at[1], u.at[depth + 1], 2, to_prev), has_prev, has_next),
        (remote(d.at[1], d.at[depth + 1], 3, to_prev), has_prev, has_next),
    ]
    y_first = [
        (remote(ys.at[1], yr.at[0], 4, to_right), has_right, has_left),
        (remote(ys.at[0], yr.at[1], 5, to_left), has_left, has_right),
    ]
    x_first = [
        (remote(xs.at[1], xr.at[0], 6, to_up), None, None),
        (remote(xs.at[0], xr.at[1], 7, to_down), None, None),
    ]
    z_second = [
        (remote(h.at[last], h.at[0], 8, to_next), has_next, has_prev),
        (remote(h.at[1], h.at[depth + 1], 9, to_prev), has_prev, has_next),
    ]
    y_second = [
        (remote(ys2.at[1], yr2.at[0], 10, to_right), has_right, has_left),
        (remote(ys2.at[0], yr2.at[1], 11, to_left), has_left, has_right),
    ]
    x_second = [
        (remote(xs2.at[1], xr2.at[0], 12, to_up), None, None),
        (remote(xs2.at[0], xr2.at[1], 13, to_down), None, None),
    ]

    def only(cond, act):
        if cond is None:
            act()
        else:
            pl.when(cond)(act)

    def start(copies):
        for copy, sends, _ in copies:
            only(sends, copy.start)

    def arrive(copies):
        for copy, _, receives in copies:
            only(receives, copy.wait_recv)

    def left_here(copies):
        for copy, sends, _ in copies:
            only(sends, copy.wait_send)

    waits = n_row + 1 + has_left.astype(jnp.int32) + has_right.astype(jnp.int32)
    pl.semaphore_wait(barrier, waits)
    start(y_first)
    start(z_first)
    start(x_first)

    def flux(da, db, ub, ua):
        return (da + db) * (ub - ua)

    def inner(src, dst, shift):
        def plane(z, uc, dc, fz, un, dn):
            nf = []
            for xb in range(blocks):
                a, k = uc[xb], dc[xb]
                if xb < blocks - 1:
                    at = pl.ds(SUB * xb + 1, SUB)
                    fx = flux(k, d[z, at, :], src[z, at, :], a)
                else:
                    fx = flux(k, pltpu.roll(k, SUB - 1, 0), pltpu.roll(a, SUB - 1, 0), a)
                    fx = jnp.where(sub == SUB - 1, 0.0, fx)
                if xb > 0:
                    at = pl.ds(SUB * xb - 1, SUB)
                    gx = flux(k, d[z, at, :], src[z, at, :], a)
                else:
                    gx = flux(k, pltpu.roll(k, 1, 0), pltpu.roll(a, 1, 0), a)
                    gx = jnp.where(sub == 0, 0.0, gx)
                fy = flux(k, pltpu.roll(k, LANES - 1, 1), pltpu.roll(a, LANES - 1, 1), a)
                fy = jnp.where(lane == LANES - 1, 0.0, fy)
                total = (fx + gx) + (fy - pltpu.roll(fy, 1, 1))
                if un is not None:
                    nz = flux(k, dn[xb], un[xb], a)
                    total = total + (nz - fz[xb])
                    nf.append(nz)
                else:
                    total = total - fz[xb]
                dst[z + shift, rows(xb), :] = a + total
            return tuple(nf)

        def load(ref, z):
            return tuple(ref[z, rows(xb), :] for xb in range(blocks))

        def step(z, carry):
            uc, dc, fz = carry
            un, dn = load(src, z + 1), load(d, z + 1)
            return un, dn, plane(z, uc, dc, fz, un, dn)

        first = (load(src, 1), load(d, 1), (zero,) * blocks)
        uc, dc, fz = lax.fori_loop(1, last, step, first)
        plane(last, uc, dc, fz, None, None)

    def x_faces(dst, first, own, came):
        for side in (0, 1):
            for k in range(chunks):
                at = pl.ds(SUB * k, SUB)
                flat, where = edge(dst, first, k, side)
                flat[where, :] = flat[where, :] + flux(
                    xs[side, 1, at, :], xr[side, 1, at, :], came(side, at), own(side, at)
                )

    def y_faces(own, came):
        even, odd = [], []
        for g in range(groups):
            at = pl.ds(SUB * g, SUB)
            a = flux(ys[0, 1, at, :], yr[0, 1, at, :], came(0, at), own(0, at))
            b = flux(ys[1, 1, at, :], yr[1, 1, at, :], came(1, at), own(1, at))
            b = pltpu.roll(b, LANES - 1, 1)
            even.append(jnp.where(is_even, a, b))
            odd.append(jnp.where(is_even, b, a))
        return even, odd

    def from_sides(packed, z0, parity, xb):
        m = spot(z0, xb)
        r = pltpu.roll(packed[parity][xb // per_group], lax.rem(LANES - m, LANES), 1)
        return jnp.where(at_ends, r, 0.0)

    inner(u, h, 0)

    arrive(x_first)
    x_faces(h, 1, lambda s, at: xs[s, 0, at, :], lambda s, at: xr[s, 0, at, :])
    arrive(y_first)
    packed = y_faces(lambda s, at: ys[s, 0, at, :], lambda s, at: yr[s, 0, at, :])
    arrive(z_first)
    for z, ghost in ((1, 0), (last, depth + 1)):
        for xb in range(blocks):
            at = rows(xb)
            fz = flux(d[z, at, :], d[ghost, at, :], u[ghost, at, :], u[z, at, :])
            h[z, at, :] = h[z, at, :] + fz + from_sides(packed, z - 1, (z - 1) % 2, xb)
    start(z_second)

    def pack_plane(z0, parity, carry, corrected):
        lh, rh = [list(c) for c in carry]
        for xb in range(blocks):
            v = h[z0 + 1, rows(xb), :]
            if not corrected:
                v = v + from_sides(packed, z0, parity, xb)
                h[z0 + 1, rows(xb), :] = v
            put((lh, rh), v, spot(z0, xb), xb)
        return tuple(lh), tuple(rh)

    def pack_pair(j, carry):
        carry = pack_plane(2 * j + 1, 1, carry, False)
        return pack_plane(2 * j + 2, 0, carry, False)

    carry = pack_plane(0, 0, (empty, empty), True)
    carry = lax.fori_loop(0, depth // 2 - 1, pack_pair, carry)
    lh, rh = pack_plane(depth - 1, 1, carry, True)
    for g in range(groups):
        at = pl.ds(SUB * g, SUB)
        ys2[0, at, :] = lh[g]
        ys2[1, at, :] = pltpu.roll(rh[g], 1, 1)
    start(y_second)
    for side in (0, 1):
        for k in range(chunks):
            flat, at = edge(h, 1, k, side)
            xs2[side, pl.ds(SUB * k, SUB), :] = flat[at, :]
    start(x_second)

    inner(h, f, -1)

    load_k.wait()
    scale = 0.5 / (depth * n_row)
    k0, k1, k2 = thick[0] * scale, thick[1] * scale, thick[2] * scale

    def opaque(v, lb):
        first, second = lb == 0, lb == 1
        half = jnp.where(first, k0, jnp.where(second, k1, k2))
        return half + half * jnp.tanh(0.5 * v), first, second

    arrive(x_second)
    x_faces(f, 0, lambda s, at: xs2[s, at, :], lambda s, at: xr2[s, at, :])
    arrive(y_second)
    packed2 = y_faces(lambda s, at: ys2[s, at, :], lambda s, at: yr2[s, at, :])

    def march(z0, parity, carry):
        through, w0, w1, w2 = [list(c) for c in carry]
        for xb in range(blocks):
            v = f[z0, rows(xb), :] + from_sides(packed2, z0, parity, xb)
            f[z0, rows(xb), :] = v
            a, first, second = opaque(v, lab[z0, rows(xb), :])
            w = through[xb] * a
            through[xb] = through[xb] - w
            w0[xb] = w0[xb] + jnp.where(first, w, 0.0)
            w1[xb] = w1[xb] + jnp.where(second, w, 0.0)
            w2[xb] = w2[xb] + jnp.where(first | second, 0.0, w)
        return tuple(tuple(c) for c in (through, w0, w1, w2))

    def march_pair(j, carry):
        return march(2 * j + 2, 0, march(2 * j + 1, 1, carry))

    one = jnp.ones((SUB, LANES), jnp.float32)
    state = ((one,) * blocks,) + ((zero,) * blocks,) * 3
    state = lax.fori_loop(0, depth // 2 - 1, march_pair, state)
    for i in range(4):
        for xb in range(blocks):
            mid[i, rows(xb), :] = state[i][xb]
    store_mid = pltpu.make_async_copy(f.at[pl.ds(1, depth - 2)], out_hbm.at[pl.ds(1, depth - 2)], lsem.at[0])
    store_mid.start()
    load_p.wait()

    arrive(z_second)
    for z0, ghost, parity in ((0, 0, 0), (depth - 1, depth + 1, 1)):
        for xb in range(blocks):
            at = rows(xb)
            fz = flux(d[z0 + 1, at, :], d[ghost, at, :], h[ghost, at, :], h[z0 + 1, at, :])
            f[z0, at, :] = f[z0, at, :] + fz + from_sides(packed2, z0, parity, xb)
    store_a = pltpu.make_async_copy(f.at[0], out_hbm.at[0], lsem.at[1])
    store_b = pltpu.make_async_copy(f.at[depth - 1], out_hbm.at[depth - 1], lsem.at[2])
    store_a.start()
    store_b.start()

    def finish(dest, ref, slot):
        at = pl.ds(pl.multiple_of(dest * SUB, SUB), SUB)
        a, fa, fb = opaque(f[0, at, :], lab[0, at, :])
        b, ga, gb = opaque(f[depth - 1, at, :], lab[depth - 1, at, :])
        clear = 1.0 - a
        through = clear * mid[0, at, :]
        w = through * b
        w0 = jnp.where(fa, a, 0.0) + clear * mid[1, at, :] + jnp.where(ga, w, 0.0)
        w1 = jnp.where(fb, a, 0.0) + clear * mid[2, at, :] + jnp.where(gb, w, 0.0)
        w2 = jnp.where(fa | fb, 0.0, a) + clear * mid[3, at, :] + jnp.where(ga | gb, 0.0, w)
        for c in range(3):
            ref[slot, c] = w0 * tint[0, c] + w1 * tint[1, c] + w2 * tint[2, c]
        ref[slot, 3] = through - w

    def hand(o):
        dest = lax.rem(me + o, n_row)
        return pltpu.make_async_remote_copy(
            src_ref=ib.at[dest], dst_ref=rb.at[me], send_sem=asem.at[o], recv_sem=bsem.at[me],
            device_id={"row": dest}, device_id_type=MESH,
        )

    for o in range(1, n_row):
        finish(lax.rem(me + o, n_row), ib, lax.rem(me + o, n_row))
        hand(o).start()
    finish(me, rb, me)

    for s in range(n_row):
        @pl.when(me != s)
        def _():
            pltpu.make_async_remote_copy(
                src_ref=ib.at[s], dst_ref=rb.at[s], send_sem=asem.at[0], recv_sem=bsem.at[s],
                device_id={"row": s}, device_id_type=MESH,
            ).wait_recv()

    through = one
    colour = [zero] * 3
    for s in range(n_row):
        for c in range(3):
            colour[c] = colour[c] + through * rb[s, c]
        through = through * rb[s, 3]
    for c in range(3):
        pic_ref[c] = colour[c]
    pic_ref[3] = 1.0 - through

    for o in range(1, n_row):
        hand(o).wait_send()
    for copies in (z_first, y_first, x_first, z_second, y_second, x_second):
        left_here(copies)
    store_mid.wait()
    store_a.wait()
    store_b.wait()


def solution(mesh):
    sizes = (mesh.shape["sx"], mesh.shape["sy"], mesh.shape["row"])
    n_row = sizes[2]

    def per_device(thermal_state, substance_label, thermal_coefficients, optical_thickness, substance_colours):
        depth, wide, tall = thermal_state.shape
        f32 = jnp.float32
        sides = (2, SUB * (depth * wide // (SUB * LANES)), LANES)
        both = (2, 2) + sides[1:]
        anywhere = pl.BlockSpec(memory_space=pl.ANY)
        return pl.pallas_call(
            functools.partial(kernel, sizes),
            out_shape=(
                jax.ShapeDtypeStruct((depth, wide, tall), f32),
                jax.ShapeDtypeStruct((4, wide // n_row, tall), f32),
            ),
            in_specs=[anywhere] * 5,
            out_specs=(anywhere, pl.BlockSpec(memory_space=pltpu.VMEM)),
            scratch_shapes=[
                pltpu.VMEM((depth + 2, wide, tall), f32),
                pltpu.VMEM((depth + 2, wide, tall), f32),
                pltpu.VMEM((depth + 2, wide, tall), f32),
                pltpu.VMEM((depth, wide, tall), f32),
                pltpu.VMEM((depth, wide, tall), jnp.int32),
                pltpu.VMEM((2, 2, depth, tall), f32),
                pltpu.VMEM((2, 2, depth, tall), f32),
                pltpu.VMEM((2, depth, tall), f32),
                pltpu.VMEM((2, depth, tall), f32),
                pltpu.VMEM(both, f32),
                pltpu.VMEM(both, f32),
                pltpu.VMEM(sides, f32),
                pltpu.VMEM(sides, f32),
                pltpu.VMEM((4, wide, tall), f32),
                pltpu.VMEM((n_row, 4, wide // n_row, tall), f32),
                pltpu.VMEM((n_row, 4, wide // n_row, tall), f32),
                pltpu.SMEM((3,), f32),
                pltpu.SMEM((3,), f32),
                pltpu.SMEM((3, 3), f32),
                pltpu.SemaphoreType.DMA((5,)),
                pltpu.SemaphoreType.DMA((14,)),
                pltpu.SemaphoreType.DMA((14,)),
                pltpu.SemaphoreType.DMA((n_row,)),
                pltpu.SemaphoreType.DMA((n_row,)),
            ],
            compiler_params=pltpu.CompilerParams(collective_id=0, has_side_effects=True),
        )(thermal_state, substance_label, thermal_coefficients, optical_thickness, substance_colours)

    placed = (P("row", "sx", "sy"), P("row", "sx", "sy"), P(), P(), P())
    return jax.shard_map(
        per_device,
        mesh=mesh,
        in_specs=placed,
        out_specs=(P("row", "sx", "sy"), P(None, ("sx", "row"), "sy")),
        check_vma=False,
    )
```

time: 126 us -> 31.1 us (0.25)
  starting transfers between devices: 37.6 us -> 0 us
  other arithmetic: 34.1 us -> 0 us
  Pallas kernels: 0 us -> 27.4 us
  waiting for transfers between devices: 26.5 us -> 0 us
  local copies, waits for them, and re-layouts: 26.2 us -> 2.92 us
    ppermute x15 -> x0, starting transfers between devices: 37.6 us -> none  [the longest x6 19.4 us: padded(): lax.ppermute(tail, axis, [(i, (i + 1) % count) for i in range(ends)])]
    pallas_call x0 -> x1, Pallas kernels: none -> 27.4 us  [per_device(): pl.pallas_call(functools.partial(kernel, sizes), out_shape=(jax.ShapeDtyp...]
    ppermute x15 -> x0, waiting for transfers between devices: 26.5 us -> none  [the longest x6 11.8 us: padded(): lax.ppermute(head, axis, [((i + 1) % count, i) for i in range(ends)])]
    slice x12 -> x0, local copies, waits for them, and re-layouts: 16.3 us -> none  [the longest x5 7.74 us: padded(): lax.slice_in_dim(cells, cells.shape[dim] - width, cells.shape[dim], axis=...]
    ppermute x4 -> x0, local copies, waits for them, and re-layouts: 8.37 us -> none  [the longest x2 5.23 us: padded(): lax.ppermute(tail, axis, [(i, (i + 1) % count) for i in range(ends)])]
    reduce_sum x1 -> x0, other arithmetic: 8.34 us -> none  [per_device(): jnp.sum(weight * lookup(substance_label, substance_colours[:, channel]),...]
    another operation x3 -> x0, other arithmetic: 6.72 us -> none  [the longest x1 4.26 us: per_device(): stacked = jnp.stack([present_warmth, coupling_operator])]
    concatenate x6 -> x0, other arithmetic: 5.52 us -> none  [the longest x3 4.9 us: padded(): jnp.concatenate([lax.ppermute(tail, axis, [(i, (i + 1) % count) for i in...]
  transfers between devices with their start and end apart: 15 -> 0, of which waited for: 10 -> 0; matrix products, arithmetic and copies ran while one was open for 7% -> 0% of each run, Pallas kernels for 0% -> 0%
where the time goes in v1:
time: 31.1 us; the launch traced here: 30.9 us
  Pallas kernels  27.4 us (88%)
  local copies, waits for them, and re-layouts  2.92 us (9%)
  between operations  0.65 us (2%)
    pallas_call x1, Pallas kernels, per_device(): pl.pallas_call(functools.partial(kernel, sizes), out_shape=(jax.ShapeDtyp...  27.4 us
    unnamed x4, local copies, waits for them, and re-layouts  2.92 us

profile of v1, /device:TPU:64, one launch (start us, length us, event | category | flops | bytes accessed | tf_op | source)
XLA Modules:
  0.0 30.9 jit_solution(16388546561518690442)
XLA Ops:
  0.6 27.4 %shard_map.68 = (f32[32,64,128]{2,1,0:T(8,128)}, f32[4,8,128]{2,1,0:T(8,128)}) custom-call(f32[32,64,128]{2,1,0:T(8,128)} %t_hbm.1, s32[32,64,128]{2,1,0:T(8,128)} %lab_hbm.1, f32[3]{0:T(128)} %coef_hbm.1, f32[3]{0:T(128)} %thick_hbm.1, f32[3,3]{1,0:T(4,128)} %tint_hbm.1), custom_call_target="tpu_custom_call" | custom-call | tf_op jit(solution)/shard_map/pallas_call | solution.py:423
  28.0 0.0 copy-start
  28.0 2.3 %copy.9 = f32[32,64,128]{2,1,0:T(8,128)} copy(f32[32,64,128]{2,1,0:T(8,128)} %get-tuple-element.4) | data formatting | bytes 2097152
  30.3 0.0 copy-done
  30.3 0.6 %copy.10 = f32[4,8,128]{2,1,0:T(8,128)} copy(f32[4,8,128]{2,1,0:T(8,128)S(1)} %copy-done) | data formatting | bytes 32768
Async XLA Ops:
  28.0 2.3 %copy-start = (f32[4,8,128]{2,1,0:T(8,128)S(1)}, f32[4,8,128]{2,1,0:T(8,128)}, u32[]{:S(2)}) copy-start(f32[4,8,128]{2,1,0:T(8,128)} %get-tuple-element.5) | copy-start | bytes 49156

commit v2 on v1

v2 whole, which is shorter than its diff:
```python
import functools

import jax
import jax.numpy as jnp
from jax import lax
from jax.experimental import pallas as pl
from jax.experimental.pallas import tpu as pltpu
from jax.sharding import PartitionSpec as P

MESH = pl.DeviceIdType.MESH
SUB, LANES = 8, 128
UNROLL, MARCH = 8, 10
VMEM_LIMIT = 16 << 20


def kernel(
    sizes,
    t_hbm, lab_hbm, coef_hbm, thick_hbm, tint_hbm,
    f, pic_ref,
    u, d, h, lab, xs, xr, xs2, xr2, fx, ys, yr, ys2, yr2, mid, ib, rb,
    coef, thick, tint, lsem, csem, ssem, rsem, asem, bsem,
):
    n_sx, n_sy, n_row = sizes
    depth, wide = lab.shape[0], lab.shape[1]
    blocks = wide // SUB
    per_group = LANES // depth
    groups = blocks // per_group
    chunks = depth // SUB
    last = depth
    me, my_sx, my_sy = lax.axis_index("row"), lax.axis_index("sx"), lax.axis_index("sy")
    has_prev, has_next = me > 0, me < n_row - 1
    has_left, has_right = my_sy > 0, my_sy < n_sy - 1

    def load(j):
        at = pl.ds(SUB * j, SUB)
        return (
            pltpu.make_async_copy(lab_hbm.at[at], lab.at[at], lsem.at[0, j]),
            pltpu.make_async_copy(t_hbm.at[at], u.at[pl.ds(SUB * j + 1, SUB)], lsem.at[1, j]),
        )

    load_c = pltpu.make_async_copy(coef_hbm, coef, csem.at[0])
    load_k = pltpu.make_async_copy(thick_hbm, thick, csem.at[1])
    load_p = pltpu.make_async_copy(tint_hbm, tint, csem.at[2])
    load_c.start()
    for j in range(chunks):
        for copy in load(j):
            copy.start()
    load_k.start()
    load_p.start()

    barrier = pltpu.get_barrier_semaphore()
    for o in range(1, n_row):
        pl.semaphore_signal(barrier, inc=1, device_id={"row": lax.rem(me + o, n_row)}, device_id_type=MESH)
    sx_next = lax.rem(my_sx + 1, n_sx)
    sx_prev = lax.rem(my_sx + n_sx - 1, n_sx)
    pl.semaphore_signal(barrier, inc=1, device_id={"sx": sx_next}, device_id_type=MESH)
    pl.semaphore_signal(barrier, inc=1, device_id={"sx": sx_prev}, device_id_type=MESH)

    @pl.when(has_left)
    def _():
        pl.semaphore_signal(barrier, inc=1, device_id={"sy": my_sy - 1}, device_id_type=MESH)

    @pl.when(has_right)
    def _():
        pl.semaphore_signal(barrier, inc=1, device_id={"sy": my_sy + 1}, device_id_type=MESH)

    lane = lax.broadcasted_iota(jnp.int32, (SUB, LANES), 1)
    sub = lax.broadcasted_iota(jnp.int32, (SUB, LANES), 0)
    at_ends = (lane == 0) | (lane == LANES - 1)
    is_even = (lane & 1) == 0
    pair = (((lane + 1) >> 1) & (LANES // 2 - 1), lane >> 1)
    zero = jnp.zeros((SUB, LANES), jnp.float32)

    @pl.when(jnp.logical_not(has_prev))
    def _():
        for a in (u, d, h):
            a[0] = jnp.zeros((wide, LANES), jnp.float32)

    @pl.when(jnp.logical_not(has_next))
    def _():
        for a in (u, d, h):
            a[depth + 1] = jnp.zeros((wide, LANES), jnp.float32)

    @pl.when(jnp.logical_not(has_left))
    def _():
        yr[0] = jnp.zeros(yr.shape[1:], jnp.float32)
        yr2[0] = jnp.zeros(yr2.shape[1:], jnp.float32)

    @pl.when(jnp.logical_not(has_right))
    def _():
        yr[1] = jnp.zeros(yr.shape[1:], jnp.float32)
        yr2[1] = jnp.zeros(yr2.shape[1:], jnp.float32)

    def rows(xb):
        return pl.ds(SUB * xb, SUB)

    def spot(z0, xb):
        return depth * (xb % per_group) + z0

    def put(acc, v, z0, parity, xb):
        m = spot(z0, xb)
        at = (parity, xb // per_group)
        acc[at] = jnp.where(pair[parity] == m >> 1, pltpu.roll(v, m, 1), acc[at])

    def fresh():
        return {(p, g): zero for p in (0, 1) for g in range(groups)}

    def faces(acc, g):
        low = jnp.where(is_even, acc[0, g], acc[1, g])
        high = jnp.where(is_even, acc[1, g], acc[0, g])
        return low, pltpu.roll(high, 1, 1)

    load_c.wait()
    c0, c1, c2 = 0.5 * coef[0], 0.5 * coef[1], 0.5 * coef[2]

    def pack_first(j, carry):
        au, ad = [dict(c) for c in carry]
        for copy in load(j):
            copy.wait()
        for i in range(SUB):
            z0 = SUB * j + i
            for xb in range(blocks):
                v = u[z0 + 1, rows(xb), :]
                lb = lab[z0, rows(xb), :]
                dv = jnp.where(lb == 0, c0, jnp.where(lb == 1, c1, c2))
                d[z0 + 1, rows(xb), :] = dv
                put(au, v, z0, i % 2, xb)
                put(ad, dv, z0, i % 2, xb)
        return au, ad

    au, ad = lax.fori_loop(0, chunks, pack_first, (fresh(), fresh()))
    for g in range(groups):
        at = pl.ds(SUB * g, SUB)
        ys[0, 0, at, :], ys[1, 0, at, :] = faces(au, g)
        ys[0, 1, at, :], ys[1, 1, at, :] = faces(ad, g)

    def edge(ref, first, k, side):
        flat = ref.reshape(ref.shape[0] * wide, LANES)
        got = None
        for i in range(SUB):
            row = flat[pl.ds((first + SUB * k + i) * wide + (wide - 1) * side, SUB, stride=0), :]
            got = row if got is None else jnp.where(sub == i, row, got)
        return got

    for side in (0, 1):
        for k in range(chunks):
            for i, a in enumerate((u, d)):
                xs[side, i, pl.ds(SUB * k, SUB), :] = edge(a, 1, k, side)

    def remote(src, dst, s, where):
        return pltpu.make_async_remote_copy(
            src_ref=src, dst_ref=dst, send_sem=ssem.at[s], recv_sem=rsem.at[s],
            device_id=where, device_id_type=MESH,
        )

    to_next, to_prev = {"row": me + 1}, {"row": me - 1}
    to_right, to_left = {"sy": my_sy + 1}, {"sy": my_sy - 1}
    to_up, to_down = {"sx": sx_next}, {"sx": sx_prev}
    z_first = [
        (remote(u.at[last], u.at[0], 0, to_next), has_next, has_prev),
        (remote(d.at[last], d.at[0], 1, to_next), has_next, has_prev),
        (remote(u.at[1], u.at[depth + 1], 2, to_prev), has_prev, has_next),
        (remote(d.at[1], d.at[depth + 1], 3, to_prev), has_prev, has_next),
    ]
    y_first = [
        (remote(ys.at[1], yr.at[0], 4, to_right), has_right, has_left),
        (remote(ys.at[0], yr.at[1], 5, to_left), has_left, has_right),
    ]
    x_first = [
        (remote(xs.at[1], xr.at[0], 6, to_up), None, None),
        (remote(xs.at[0], xr.at[1], 7, to_down), None, None),
    ]
    z_second = [
        (remote(h.at[last], h.at[0], 8, to_next), has_next, has_prev),
        (remote(h.at[1], h.at[depth + 1], 9, to_prev), has_prev, has_next),
    ]
    y_second = [
        (remote(ys2.at[1], yr2.at[0], 10, to_right), has_right, has_left),
        (remote(ys2.at[0], yr2.at[1], 11, to_left), has_left, has_right),
    ]
    x_second = [
        (remote(xs2.at[1], xr2.at[0], 12, to_up), None, None),
        (remote(xs2.at[0], xr2.at[1], 13, to_down), None, None),
    ]

    def only(cond, act):
        if cond is None:
            act()
        else:
            pl.when(cond)(act)

    def start(copies):
        for copy, sends, _ in copies:
            only(sends, copy.start)

    def arrive(copies):
        for copy, _, receives in copies:
            only(receives, copy.wait_recv)

    def left_here(copies):
        for copy, sends, _ in copies:
            only(sends, copy.wait_send)

    waits = n_row + 1 + has_left.astype(jnp.int32) + has_right.astype(jnp.int32)
    pl.semaphore_wait(barrier, waits)
    start(y_first)
    start(z_first)
    start(x_first)

    def flux(da, db, ub, ua):
        return (da + db) * (ub - ua)

    def inner(src, dst, shift):
        def plane(z, fz, closing):
            nf, before = [], None
            for xb in range(blocks):
                a, k = src[z, rows(xb), :], d[z, rows(xb), :]
                if xb < blocks - 1:
                    at = pl.ds(SUB * xb + 1, SUB)
                    fxx = flux(k, d[z, at, :], src[z, at, :], a)
                else:
                    fxx = flux(k, pltpu.roll(k, SUB - 1, 0), pltpu.roll(a, SUB - 1, 0), a)
                    fxx = jnp.where(sub == SUB - 1, 0.0, fxx)
                turned = pltpu.roll(fxx, 1, 0)
                behind = jnp.where(sub == 0, 0.0 if before is None else before, turned)
                before = turned
                fy = flux(k, pltpu.roll(k, LANES - 1, 1), pltpu.roll(a, LANES - 1, 1), a)
                total = (fxx - behind) + (fy - pltpu.roll(fy, 1, 1))
                if not closing:
                    nz = flux(k, d[z + 1, rows(xb), :], src[z + 1, rows(xb), :], a)
                    total = total + (nz - fz[xb])
                    nf.append(nz)
                else:
                    total = total - fz[xb]
                dst[z + shift, rows(xb), :] = a + total
            return tuple(nf)

        def several(j, fz):
            for i in range(UNROLL):
                fz = plane(UNROLL * j + 1 + i, fz, False)
            return fz

        fz = lax.fori_loop(0, depth // UNROLL - 1, several, (zero,) * blocks)
        for z in range(depth - UNROLL + 1, depth + 1):
            fz = plane(z, fz, z == last)

    def x_faces(own, came):
        for side in (0, 1):
            for k in range(chunks):
                at = pl.ds(SUB * k, SUB)
                fx[side, at, :] = flux(xs[side, 1, at, :], xr[side, 1, at, :], came(side, at), own(side, at))

    def y_faces(own, came):
        even, odd = [], []
        for g in range(groups):
            at = pl.ds(SUB * g, SUB)
            dl, dr, ul, ur = ys[0, 1, at, :], ys[1, 1, at, :], own(0, at), own(1, at)
            closed = flux(dl, dr, ul, ur)
            a = flux(dl, yr[0, 1, at, :], came(0, at), ul) + closed
            b = flux(dr, yr[1, 1, at, :], came(1, at), ur) - closed
            b = pltpu.roll(b, LANES - 1, 1)
            even.append(jnp.where(is_even, a, b))
            odd.append(jnp.where(is_even, b, a))
        return even, odd

    def with_faces(v, packed, z0, parity, xb):
        r = pltpu.roll(packed[parity][xb // per_group], (LANES - spot(z0, xb)) & (LANES - 1), 1)
        v = jnp.where(at_ends, v + r, v)
        if xb == 0:
            v = jnp.where(sub == 0, v + fx[0, pl.ds(z0, SUB, stride=0), :], v)
        if xb == blocks - 1:
            v = jnp.where(sub == SUB - 1, v + fx[1, pl.ds(z0, SUB, stride=0), :], v)
        return v

    inner(u, h, 0)

    arrive(x_first)
    x_faces(lambda s, at: xs[s, 0, at, :], lambda s, at: xr[s, 0, at, :])
    arrive(y_first)
    packed = y_faces(lambda s, at: ys[s, 0, at, :], lambda s, at: yr[s, 0, at, :])

    def correct(z0, parity, acc):
        for xb in range(blocks):
            v = with_faces(h[z0 + 1, rows(xb), :], packed, z0, parity, xb)
            h[z0 + 1, rows(xb), :] = v
            put(acc, v, z0, parity, xb)

    def correct_some(j, acc):
        acc = dict(acc)
        for i in range(MARCH):
            correct(MARCH * j + 1 + i, (1 + i) % 2, acc)
        return acc

    acc = dict(lax.fori_loop(0, (depth - 2) // MARCH, correct_some, fresh()))
    arrive(z_first)
    for z0, ghost, parity in ((0, 0, 0), (depth - 1, depth + 1, 1)):
        for xb in range(blocks):
            at = rows(xb)
            fz = flux(d[z0 + 1, at, :], d[ghost, at, :], u[ghost, at, :], u[z0 + 1, at, :])
            v = with_faces(h[z0 + 1, at, :] + fz, packed, z0, parity, xb)
            h[z0 + 1, at, :] = v
            put(acc, v, z0, parity, xb)
    start(z_second)
    for g in range(groups):
        at = pl.ds(SUB * g, SUB)
        ys2[0, at, :], ys2[1, at, :] = faces(acc, g)
    start(y_second)
    for side in (0, 1):
        for k in range(chunks):
            xs2[side, pl.ds(SUB * k, SUB), :] = edge(h, 1, k, side)
    start(x_second)

    inner(h, f, -1)

    load_k.wait()
    scale = 0.5 / (depth * n_row)
    k0, k1, k2 = thick[0] * scale, thick[1] * scale, thick[2] * scale

    def opaque(v, lb):
        first, second = lb == 0, lb == 1
        half = jnp.where(first, k0, jnp.where(second, k1, k2))
        return half + half * jnp.tanh(0.5 * v), first, second

    arrive(x_second)
    x_faces(lambda s, at: xs2[s, at, :], lambda s, at: xr2[s, at, :])
    arrive(y_second)
    packed2 = y_faces(lambda s, at: ys2[s, at, :], lambda s, at: yr2[s, at, :])

    def march(z0, parity, carry):
        through, w0, w1 = [list(c) for c in carry]
        for xb in range(blocks):
            v = with_faces(f[z0, rows(xb), :], packed2, z0, parity, xb)
            f[z0, rows(xb), :] = v
            a, first, second = opaque(v, lab[z0, rows(xb), :])
            w = through[xb] * a
            through[xb] = through[xb] - w
            w0[xb] = w0[xb] + jnp.where(first, w, 0.0)
            w1[xb] = w1[xb] + jnp.where(second, w, 0.0)
        return tuple(tuple(c) for c in (through, w0, w1))

    def march_some(j, carry):
        for i in range(MARCH):
            carry = march(MARCH * j + 1 + i, (1 + i) % 2, carry)
        return carry

    one = jnp.ones((SUB, LANES), jnp.float32)
    state = ((one,) * blocks,) + ((zero,) * blocks,) * 2
    state = lax.fori_loop(0, (depth - 2) // MARCH, march_some, state)
    for i in range(3):
        for xb in range(blocks):
            mid[i, rows(xb), :] = state[i][xb]
    load_p.wait()

    arrive(z_second)
    for xb in range(blocks):
        at = rows(xb)
        ends = []
        for z0, ghost, parity in ((0, 0, 0), (depth - 1, depth + 1, 1)):
            fz = flux(d[z0 + 1, at, :], d[ghost, at, :], h[ghost, at, :], h[z0 + 1, at, :])
            v = with_faces(f[z0, at, :] + fz, packed2, z0, parity, xb)
            f[z0, at, :] = v
            ends.append(opaque(v, lab[z0, at, :]))
        (a, fa, fb), (b, ga, gb) = ends
        clear = 1.0 - a
        through = clear * mid[0, at, :]
        w = through * b
        ib[xb, 0] = jnp.where(fa, a, 0.0) + clear * mid[1, at, :] + jnp.where(ga, w, 0.0)
        ib[xb, 1] = jnp.where(fb, a, 0.0) + clear * mid[2, at, :] + jnp.where(gb, w, 0.0)
        ib[xb, 2] = through - w

    def hand(o):
        dest = lax.rem(me + o, n_row)
        return pltpu.make_async_remote_copy(
            src_ref=ib.at[dest], dst_ref=rb.at[me], send_sem=asem.at[o], recv_sem=bsem.at[me],
            device_id={"row": dest}, device_id_type=MESH,
        )

    for o in range(1, n_row):
        hand(o).start()
    rb[me] = ib[me]

    for s in range(n_row):
        @pl.when(me != s)
        def _():
            pltpu.make_async_remote_copy(
                src_ref=ib.at[s], dst_ref=rb.at[s], send_sem=asem.at[0], recv_sem=bsem.at[s],
                device_id={"row": s}, device_id_type=MESH,
            ).wait_recv()

    through, w0, w1 = one, zero, zero
    for s in range(n_row):
        w0 = w0 + through * rb[s, 0]
        w1 = w1 + through * rb[s, 1]
        through = through * rb[s, 2]
    blocked = 1.0 - through
    w2 = (blocked - w0) - w1
    for c in range(3):
        pic_ref[c] = w0 * tint[0, c] + w1 * tint[1, c] + w2 * tint[2, c]
    pic_ref[3] = blocked

    for o in range(1, n_row):
        hand(o).wait_send()
    for copies in (z_first, y_first, x_first, z_second, y_second, x_second):
        left_here(copies)


def deliver(f, pic, out, out_pic, sem):
    a = pltpu.make_async_copy(f, out, sem.at[0])
    b = pltpu.make_async_copy(pic, out_pic, sem.at[1])
    a.start()
    b.start()
    a.wait()
    b.wait()


def solution(mesh):
    sizes = (mesh.shape["sx"], mesh.shape["sy"], mesh.shape["row"])
    n_row = sizes[2]

    def per_device(thermal_state, substance_label, thermal_coefficients, optical_thickness, substance_colours):
        depth, wide, tall = thermal_state.shape
        f32 = jnp.float32
        sides = (2, SUB * (depth * wide // (SUB * LANES)), LANES)
        both = (2, 2) + sides[1:]
        anywhere = pl.BlockSpec(memory_space=pl.ANY)
        near = pl.BlockSpec(memory_space=pltpu.VMEM)
        chunks = depth // SUB
        results = (
            jax.ShapeDtypeStruct((depth, wide, tall), f32),
            jax.ShapeDtypeStruct((4, wide // n_row, tall), f32),
        )
        f, pic = pl.pallas_call(
            functools.partial(kernel, sizes),
            out_shape=results,
            in_specs=[pl.BlockSpec(memory_space=pltpu.HBM)] * 5,
            out_specs=(near, near),
            scratch_shapes=[
                pltpu.VMEM((depth + 2, wide, tall), f32),
                pltpu.VMEM((depth + 2, wide, tall), f32),
                pltpu.VMEM((depth + 2, wide, tall), f32),
                pltpu.VMEM((depth, wide, tall), jnp.int32),
                pltpu.VMEM((2, 2, depth, tall), f32),
                pltpu.VMEM((2, 2, depth, tall), f32),
                pltpu.VMEM((2, depth, tall), f32),
                pltpu.VMEM((2, depth, tall), f32),
                pltpu.VMEM((2, depth, tall), f32),
                pltpu.VMEM(both, f32),
                pltpu.VMEM(both, f32),
                pltpu.VMEM(sides, f32),
                pltpu.VMEM(sides, f32),
                pltpu.VMEM((3, wide, tall), f32),
                pltpu.VMEM((n_row, 3, wide // n_row, tall), f32),
                pltpu.VMEM((n_row, 3, wide // n_row, tall), f32),
                pltpu.SMEM((3,), f32),
                pltpu.SMEM((3,), f32),
                pltpu.SMEM((3, 3), f32),
                pltpu.SemaphoreType.DMA((2, chunks)),
                pltpu.SemaphoreType.DMA((3,)),
                pltpu.SemaphoreType.DMA((14,)),
                pltpu.SemaphoreType.DMA((14,)),
                pltpu.SemaphoreType.DMA((n_row,)),
                pltpu.SemaphoreType.DMA((n_row,)),
            ],
            compiler_params=pltpu.CompilerParams(
                collective_id=0, has_side_effects=True, vmem_limit_bytes=VMEM_LIMIT
            ),
        )(*[pltpu.with_memory_space_constraint(a, pltpu.HBM) for a in (thermal_state, substance_label, thermal_coefficients, optical_thickness, substance_colours)])
        return pl.pallas_call(
            deliver,
            out_shape=results,
            in_specs=[near, near],
            out_specs=(anywhere, anywhere),
            scratch_shapes=[pltpu.SemaphoreType.DMA((2,))],
            compiler_params=pltpu.CompilerParams(vmem_limit_bytes=VMEM_LIMIT),
        )(f, pic)

    placed = (P("row", "sx", "sy"), P("row", "sx", "sy"), P(), P(), P())
    return jax.shard_map(
        per_device,
        mesh=mesh,
        in_specs=placed,
        out_specs=(P("row", "sx", "sy"), P(None, ("sx", "row"), "sy")),
        check_vma=False,
    )
```

time: 31.1 us -> 26.9 us (0.86)
  local copies, waits for them, and re-layouts: 2.92 us -> 0 us
  Pallas kernels: 27.4 us -> 26.1 us
    unnamed x4 -> x0, local copies, waits for them, and re-layouts: 2.92 us -> none
    pallas_call x1 -> x2, Pallas kernels: 27.4 us -> 26.1 us  [the longest x1 25.1 us: per_device(): pl.pallas_call(functools.partial(kernel, sizes), out_shape=results, in_sp...]
where the time goes in v2:
time: 26.9 us; the launch traced here: 26.8 us
  Pallas kernels  26.1 us (97%)
  between operations  0.64 us (2%)
    pallas_call x1, Pallas kernels, per_device(): pl.pallas_call(functools.partial(kernel, sizes), out_shape=results, in_sp...  25.1 us
    pallas_call x1, Pallas kernels, per_device(): pl.pallas_call(deliver, out_shape=results, in_specs=[near, near], out_spe...  0.99 us

profile of v2, /device:TPU:64, one launch (start us, length us, event | category | flops | bytes accessed | tf_op | source)
XLA Modules:
  0.0 26.8 jit_solution(166535072732017573)
XLA Ops:
  0.6 25.1 %shard_map.68 = (f32[32,64,128]{2,1,0:T(8,128)S(1)}, f32[4,8,128]{2,1,0:T(8,128)S(1)}) custom-call(f32[32,64,128]{2,1,0:T(8,128)} %t_hbm.1, s32[32,64,128]{2,1,0:T(8,128)} %lab_hbm.1, f32[3]{0:T(128)} %coef_hbm.1, f32[3]{0:T(128)} %thick_hbm.1, f32[3,3]{1,0:T(4,128)} %tint_hbm.1), custom_call_target="tpu_custom_call" | custom-call | tf_op jit(solution)/shard_map/pallas_call | solution.py:432
  25.8 1.0 %shard_map.69 = (f32[32,64,128]{2,1,0:T(8,128)}, f32[4,8,128]{2,1,0:T(8,128)}) custom-call(f32[32,64,128]{2,1,0:T(8,128)S(1)} %get-tuple-element.4.f, f32[4,8,128]{2,1,0:T(8,128)S(1)} %get-tuple-element.5.pic), custom_call_target="tpu_custom_call" | custom-call | tf_op jit(solution)/shard_map/pallas_call | solution.py:468

commit v3 on v2

v3 whole, which is shorter than its diff:
```python
import functools

import jax
import jax.numpy as jnp
from jax import lax
from jax.experimental import pallas as pl
from jax.experimental.pallas import tpu as pltpu
from jax.sharding import PartitionSpec as P

MESH = pl.DeviceIdType.MESH
SUB, LANES = 8, 128
FLUX, FIX, PACK, MARCH, PARTS = 4, 6, 6, 6, 4
VMEM_LIMIT = 16 << 20


def kernel(
    sizes,
    t_hbm, lab_hbm, coef_hbm, thick_hbm, tint_hbm,
    f, pic_ref,
    u, d, h, ky, fy, lab, xs, xr, xs2, xr2, xs3, xr3, fx, fx3, ys, yr, ys2, yr2, ys3, yr3, mid, ib, rb,
    coef, thick, tint, lsem, csem, zsem1, zrec1, zsem2, zrec2, ssem, rsem, asem, bsem,
):
    n_sx, n_sy, n_row = sizes
    depth, wide = t_hbm.shape[0], t_hbm.shape[1]
    blocks = wide // SUB
    per_group = LANES // depth
    groups = blocks // per_group
    chunks = depth // SUB
    last = depth
    per_part = blocks // PARTS
    me, my_sx, my_sy = lax.axis_index("row"), lax.axis_index("sx"), lax.axis_index("sy")
    has_prev, has_next = me > 0, me < n_row - 1
    has_left, has_right = my_sy > 0, my_sy < n_sy - 1

    def load(j):
        at, to = pl.ds(SUB * j, SUB), pl.ds(SUB * j + 1, SUB)
        return (
            pltpu.make_async_copy(lab_hbm.at[at], lab.at[to], lsem.at[0, j]),
            pltpu.make_async_copy(t_hbm.at[at], u.at[to], lsem.at[1, j]),
        )

    load_c = pltpu.make_async_copy(coef_hbm, coef, csem.at[0])
    load_k = pltpu.make_async_copy(thick_hbm, thick, csem.at[1])
    load_p = pltpu.make_async_copy(tint_hbm, tint, csem.at[2])
    load_c.start()
    for j in range(chunks):
        for copy in load(j):
            copy.start()
    load_k.start()
    load_p.start()

    barrier = pltpu.get_barrier_semaphore()
    for o in range(1, n_row):
        pl.semaphore_signal(barrier, inc=1, device_id={"row": lax.rem(me + o, n_row)}, device_id_type=MESH)
    sx_next = lax.rem(my_sx + 1, n_sx)
    sx_prev = lax.rem(my_sx + n_sx - 1, n_sx)
    pl.semaphore_signal(barrier, inc=1, device_id={"sx": sx_next}, device_id_type=MESH)
    pl.semaphore_signal(barrier, inc=1, device_id={"sx": sx_prev}, device_id_type=MESH)

    @pl.when(has_left)
    def _():
        pl.semaphore_signal(barrier, inc=1, device_id={"sy": my_sy - 1}, device_id_type=MESH)

    @pl.when(has_right)
    def _():
        pl.semaphore_signal(barrier, inc=1, device_id={"sy": my_sy + 1}, device_id_type=MESH)

    lane = lax.broadcasted_iota(jnp.int32, (SUB, LANES), 1)
    sub = lax.broadcasted_iota(jnp.int32, (SUB, LANES), 0)
    at_ends = (lane == 0) | (lane == LANES - 1)
    is_even = (lane & 1) == 0
    pair = (((lane + 1) >> 1) & (LANES // 2 - 1), lane >> 1)
    zero = jnp.zeros((SUB, LANES), jnp.float32)
    one = jnp.ones((SUB, LANES), jnp.float32)

    def clear(cond, refs):
        @pl.when(jnp.logical_not(cond))
        def _():
            for r in refs:
                r[...] = jnp.zeros(r.shape, r.dtype)

    clear(has_prev, (u.at[0], d.at[0], h.at[0]))
    clear(has_next, (u.at[depth + 1], d.at[depth + 1], h.at[depth + 1]))
    clear(has_left, (yr.at[0], yr2.at[0], yr3.at[0]))
    clear(has_right, (yr.at[1], yr2.at[1], yr3.at[1]))

    to_next, to_prev = {"row": me + 1}, {"row": me - 1}
    to_right, to_left = {"sy": my_sy + 1}, {"sy": my_sy - 1}
    to_up, to_down = {"sx": sx_next}, {"sx": sx_prev}

    def only(cond, act):
        if cond is None:
            act()
        else:
            pl.when(cond)(act)

    def start(copies):
        for copy, sends, _ in copies:
            only(sends, copy.start)

    def arrive(copies):
        for copy, _, receives in copies:
            only(receives, copy.wait_recv)

    def left_here(copies):
        for copy, sends, _ in copies:
            only(sends, copy.wait_send)

    def remote(src, dst, send, recv, where):
        return pltpu.make_async_remote_copy(
            src_ref=src, dst_ref=dst, send_sem=send, recv_sem=recv, device_id=where, device_id_type=MESH
        )

    def z_first(p):
        at = pl.ds(SUB * per_part * p, SUB * per_part)
        got = []
        for i, (src, dst) in enumerate(((t_hbm, u), (lab_hbm, lab))):
            got.append((remote(src.at[depth - 1, at], dst.at[0, at], zsem1.at[0, i, p], zrec1.at[0, i, p], to_next),
                        has_next, has_prev))
            got.append((remote(src.at[0, at], dst.at[depth + 1, at], zsem1.at[1, i, p], zrec1.at[1, i, p], to_prev),
                        has_prev, has_next))
        return got

    def z_second(p):
        at = pl.ds(SUB * per_part * p, SUB * per_part)
        return [
            (remote(h.at[last, at], h.at[0, at], zsem2.at[0, p], zrec2.at[0, p], to_next), has_next, has_prev),
            (remote(h.at[1, at], h.at[depth + 1, at], zsem2.at[1, p], zrec2.at[1, p], to_prev), has_prev, has_next),
        ]

    def y_copies(src, dst, s):
        return [
            (remote(src.at[1], dst.at[0], ssem.at[s], rsem.at[s], to_right), has_right, has_left),
            (remote(src.at[0], dst.at[1], ssem.at[s + 1], rsem.at[s + 1], to_left), has_left, has_right),
        ]

    def x_copies(src, dst, s):
        return [
            (remote(src.at[1], dst.at[0], ssem.at[s], rsem.at[s], to_up), None, None),
            (remote(src.at[0], dst.at[1], ssem.at[s + 1], rsem.at[s + 1], to_down), None, None),
        ]

    y_first, x_first = y_copies(ys, yr, 0), x_copies(xs, xr, 2)
    y_second, x_second = y_copies(ys2, yr2, 4), x_copies(xs2, xr2, 6)
    y_third, x_third = y_copies(ys3, yr3, 8), x_copies(xs3, xr3, 10)

    waits = n_row + 1 + has_left.astype(jnp.int32) + has_right.astype(jnp.int32)
    pl.semaphore_wait(barrier, waits)
    for p in range(PARTS):
        start(z_first(p))

    def rows(xb):
        return pl.ds(SUB * xb, SUB)

    def spot(z0, xb):
        return depth * (xb % per_group) + z0

    def put(acc, v, z0, parity, xb):
        m = spot(z0, xb)
        at = (parity, xb // per_group)
        acc[at] = jnp.where(pair[parity] == m >> 1, pltpu.roll(v, m, 1), acc[at])

    def fresh():
        return {(p, g): zero for p in (0, 1) for g in range(groups)}

    def faces(acc, g):
        low = jnp.where(is_even, acc[0, g], acc[1, g])
        high = jnp.where(is_even, acc[1, g], acc[0, g])
        return low, pltpu.roll(high, 1, 1)

    load_c.wait()
    c0, c1, c2 = 0.5 * coef[0], 0.5 * coef[1], 0.5 * coef[2]

    def conduct(lb):
        return jnp.where(lb == 0, c0, jnp.where(lb == 1, c1, c2))

    def pack_first(j, carry):
        au, ad = [dict(c) for c in carry]
        for copy in load(j):
            copy.wait()
        for i in range(SUB):
            z0 = SUB * j + i
            for xb in range(blocks):
                v = u[z0 + 1, rows(xb), :]
                dv = conduct(lab[z0 + 1, rows(xb), :])
                d[z0 + 1, rows(xb), :] = dv
                put(au, v, z0, i % 2, xb)
                put(ad, dv, z0, i % 2, xb)
        return au, ad

    au, ad = lax.fori_loop(0, chunks, pack_first, (fresh(), fresh()))
    for g in range(groups):
        at = pl.ds(SUB * g, SUB)
        ys[0, 0, at, :], ys[1, 0, at, :] = faces(au, g)
        ys[0, 1, at, :], ys[1, 1, at, :] = faces(ad, g)
    start(y_first)

    def edge(ref, first, k, side):
        flat = ref.reshape(ref.shape[0] * wide, LANES)
        got = None
        for i in range(SUB):
            row = flat[pl.ds((first + SUB * k + i) * wide + (wide - 1) * side, SUB, stride=0), :]
            got = row if got is None else jnp.where(sub == i, row, got)
        return got

    for side in (0, 1):
        for k in range(chunks):
            for i, a in enumerate((u, d)):
                xs[side, i, pl.ds(SUB * k, SUB), :] = edge(a, 1, k, side)
    start(x_first)

    def flux(da, db, ub, ua):
        return (da + db) * (ub - ua)

    def plane(src, dst, shift, z, fz, high, first_step):
        nf, before = [], None
        for xb in range(blocks):
            a, k = src[z, rows(xb), :], d[z, rows(xb), :]
            if xb < blocks - 1:
                at = pl.ds(SUB * xb + 1, SUB)
                fxx = flux(k, d[z, at, :], src[z, at, :], a)
            else:
                fxx = flux(k, pltpu.roll(k, SUB - 1, 0), pltpu.roll(a, SUB - 1, 0), a)
                fxx = jnp.where(sub == SUB - 1, 0.0, fxx)
            turned = pltpu.roll(fxx, 1, 0)
            behind = jnp.where(sub == 0, 0.0 if before is None else before, turned)
            before = turned
            if first_step:
                kk = k + pltpu.roll(k, LANES - 1, 1)
                ky[z - 1, rows(xb), :] = kk
            else:
                kk = ky[z - 1, rows(xb), :]
            gy = kk * (pltpu.roll(a, LANES - 1, 1) - a)
            fy[z - 1, rows(xb), :] = gy
            total = (fxx - behind) + gy
            if high:
                nz = flux(k, d[z + 1, rows(xb), :], src[z + 1, rows(xb), :], a)
                total = total + (nz if fz is None else nz - fz[xb])
                nf.append(nz)
            elif fz is not None:
                total = total - fz[xb]
            dst[z + shift, rows(xb), :] = a + total
        return tuple(nf)

    def between(src, z):
        return tuple(
            flux(d[z, rows(xb), :], d[z + 1, rows(xb), :], src[z + 1, rows(xb), :], src[z, rows(xb), :])
            for xb in range(blocks)
        )

    def planes(src, dst, shift, begin, count, fz, first_step):
        def several(j, fz):
            for i in range(FLUX):
                fz = plane(src, dst, shift, begin + FLUX * j + i, fz, True, first_step)
            return fz

        return lax.fori_loop(0, count // FLUX, several, fz)

    fz = plane(u, h, 0, 1, None, True, True)
    fz = planes(u, h, 0, 2, depth - FLUX, fz, True)
    for z in range(depth - FLUX + 2, last):
        fz = plane(u, h, 0, z, fz, True, True)
    plane(u, h, 0, last, fz, False, True)

    def x_faces(to, tiles, own, came):
        for side in (0, 1):
            for i, k in enumerate(tiles):
                at, place = pl.ds(SUB * k, SUB), pl.ds(SUB * i, SUB)
                to[side, place, :] = flux(
                    xs[side, 1, at, :], xr[side, 1, at, :], came(side, place), own(side, place)
                )

    def y_faces(own, came):
        even, odd = [], []
        for g in range(groups):
            at = pl.ds(SUB * g, SUB)
            dl, dr, ul, ur = ys[0, 1, at, :], ys[1, 1, at, :], own(0, at), own(1, at)
            closed = flux(dl, dr, ul, ur)
            a = flux(dl, yr[0, 1, at, :], came(0, at), ul) + closed
            b = flux(dr, yr[1, 1, at, :], came(1, at), ur) - closed
            b = pltpu.roll(b, LANES - 1, 1)
            even.append(jnp.where(is_even, a, b))
            odd.append(jnp.where(is_even, b, a))
        return even, odd

    def with_faces(v, packed, rowsx, zx, z0, parity, xb):
        r = pltpu.roll(packed[parity][xb // per_group], (LANES - spot(z0, xb)) & (LANES - 1), 1)
        v = v - pltpu.roll(fy[z0, rows(xb), :], 1, 1)
        v = jnp.where(at_ends, v + r, v)
        if xb == 0:
            v = jnp.where(sub == 0, v + rowsx[0, pl.ds(zx, SUB, stride=0), :], v)
        if xb == blocks - 1:
            v = jnp.where(sub == SUB - 1, v + rowsx[1, pl.ds(zx, SUB, stride=0), :], v)
        return v

    def sweep(count, body, carry):
        def some(j, carry):
            for i in range(count):
                carry = body(count * j + 1 + i, (1 + i) % 2, carry)
            return carry

        return lax.fori_loop(0, (depth - 2) // count, some, carry)

    arrive(x_first)
    x_faces(fx, range(chunks), lambda s, at: xs[s, 0, at, :], lambda s, at: xr[s, 0, at, :])
    arrive(y_first)
    packed = y_faces(lambda s, at: ys[s, 0, at, :], lambda s, at: yr[s, 0, at, :])

    def fix_h(z0, parity, carry):
        for xb in range(blocks):
            h[z0 + 1, rows(xb), :] = with_faces(h[z0 + 1, rows(xb), :], packed, fx, z0, z0, parity, xb)
        return carry

    def pack_h(z0, parity, acc):
        acc = dict(acc)
        for xb in range(blocks):
            put(acc, h[z0 + 1, rows(xb), :], z0, parity, xb)
        return acc

    sweep(FIX, fix_h, 0)
    acc = dict(sweep(PACK, pack_h, fresh()))

    def y_out(to, acc):
        for g in range(groups):
            at = pl.ds(SUB * g, SUB)
            to[0, at, :], to[1, at, :] = faces(acc, g)

    y_out(ys2, acc)
    start(y_second)
    for side in (0, 1):
        for k in range(chunks):
            xs2[side, pl.ds(SUB * k, SUB), :] = edge(h, 1, k, side)
    start(x_second)
    planes(h, f, -1, 3, depth - 4, between(h, 2), False)

    outer = ((0, 0, 0), (depth - 1, depth + 1, 1))
    tiles = (0, chunks - 1)

    for p in range(PARTS):
        arrive(z_first(p))
        for (z0, ghost, parity), inside in zip(outer, (has_prev, has_next)):
            for xb in range(per_part * p, per_part * (p + 1)):
                at = rows(xb)
                dg = jnp.where(inside, conduct(lab[ghost, at, :]), 0.0)
                d[ghost, at, :] = dg
                fz = flux(d[z0 + 1, at, :], dg, u[ghost, at, :], u[z0 + 1, at, :])
                h[z0 + 1, at, :] = with_faces(h[z0 + 1, at, :] + fz, packed, fx, z0, z0, parity, xb)
        start(z_second(p))

    for z0, _, parity in outer:
        acc = pack_h(z0, parity, acc)
    y_out(ys3, acc)
    start(y_third)
    for side in (0, 1):
        for i, k in enumerate(tiles):
            xs3[side, pl.ds(SUB * i, SUB), :] = edge(h, 1, k, side)
    start(x_third)

    fz = plane(h, f, -1, 1, None, True, False)
    plane(h, f, -1, 2, fz, True, False)
    fz = plane(h, f, -1, last - 1, between(h, last - 2), True, False)
    plane(h, f, -1, last, fz, False, False)

    arrive(x_second)
    x_faces(fx, range(chunks), lambda s, at: xs2[s, at, :], lambda s, at: xr2[s, at, :])
    arrive(y_second)
    packed2 = y_faces(lambda s, at: ys2[s, at, :], lambda s, at: yr2[s, at, :])

    def fix_f(z0, parity, carry):
        for xb in range(blocks):
            f[z0, rows(xb), :] = with_faces(f[z0, rows(xb), :], packed2, fx, z0, z0, parity, xb)
        return carry

    sweep(FIX, fix_f, 0)

    load_k.wait()
    scale = 0.5 / (depth * n_row)
    k0, k1, k2 = thick[0] * scale, thick[1] * scale, thick[2] * scale

    def opaque(v, lb):
        first, second = lb == 0, lb == 1
        half = jnp.where(first, k0, jnp.where(second, k1, k2))
        return half + half * jnp.tanh(0.5 * v), first, second

    def march(z0, parity, carry):
        through, w0, w1 = [list(c) for c in carry]
        for xb in range(blocks):
            a, first, second = opaque(f[z0, rows(xb), :], lab[z0 + 1, rows(xb), :])
            w = through[xb] * a
            through[xb] = through[xb] - w
            w0[xb] = w0[xb] + jnp.where(first, w, 0.0)
            w1[xb] = w1[xb] + jnp.where(second, w, 0.0)
        return tuple(tuple(c) for c in (through, w0, w1))

    state = sweep(MARCH, march, ((one,) * blocks,) + ((zero,) * blocks,) * 2)
    for i in range(3):
        for xb in range(blocks):
            mid[i, rows(xb), :] = state[i][xb]

    arrive(x_third)
    x_faces(fx3, tiles, lambda s, at: xs3[s, at, :], lambda s, at: xr3[s, at, :])
    arrive(y_third)
    packed3 = y_faces(lambda s, at: ys3[s, at, :], lambda s, at: yr3[s, at, :])
    for z0, _, parity in outer:
        for xb in range(blocks):
            f[z0, rows(xb), :] = with_faces(
                f[z0, rows(xb), :], packed3, fx3, z0 if z0 == 0 else 2 * SUB - 1, z0, parity, xb
            )
    load_p.wait()

    def hand(dest):
        return pltpu.make_async_remote_copy(
            src_ref=ib.at[dest], dst_ref=rb.at[me], send_sem=asem.at[dest], recv_sem=bsem.at[me],
            device_id={"row": dest}, device_id_type=MESH,
        )

    for p in range(PARTS):
        arrive(z_second(p))
        for xb in range(per_part * p, per_part * (p + 1)):
            at = rows(xb)
            ends = []
            for z0, ghost, parity in outer:
                fz = flux(d[z0 + 1, at, :], d[ghost, at, :], h[ghost, at, :], h[z0 + 1, at, :])
                v = f[z0, at, :] + fz
                f[z0, at, :] = v
                ends.append(opaque(v, lab[z0 + 1, at, :]))
            (a, fa, fb), (b, ga, gb) = ends
            clear_a = 1.0 - a
            through = clear_a * mid[0, at, :]
            w = through * b
            ib[xb, 0] = jnp.where(fa, a, 0.0) + clear_a * mid[1, at, :] + jnp.where(ga, w, 0.0)
            ib[xb, 1] = jnp.where(fb, a, 0.0) + clear_a * mid[2, at, :] + jnp.where(gb, w, 0.0)
            ib[xb, 2] = through - w
        for dest in range(per_part * p, per_part * (p + 1)):
            pl.when(me != dest)(hand(dest).start)
    rb[me] = ib[me]

    for s in range(n_row):
        @pl.when(me != s)
        def _():
            pltpu.make_async_remote_copy(
                src_ref=ib.at[s], dst_ref=rb.at[s], send_sem=asem.at[s], recv_sem=bsem.at[s],
                device_id={"row": s}, device_id_type=MESH,
            ).wait_recv()

    through, w0, w1 = one, zero, zero
    for s in range(n_row):
        w0 = w0 + through * rb[s, 0]
        w1 = w1 + through * rb[s, 1]
        through = through * rb[s, 2]
    blocked = 1.0 - through
    w2 = (blocked - w0) - w1
    for c in range(3):
        pic_ref[c] = w0 * tint[0, c] + w1 * tint[1, c] + w2 * tint[2, c]
    pic_ref[3] = blocked

    for dest in range(n_row):
        pl.when(me != dest)(hand(dest).wait_send)
    for p in range(PARTS):
        left_here(z_first(p))
        left_here(z_second(p))
    for copies in (y_first, x_first, y_second, x_second, y_third, x_third):
        left_here(copies)


def deliver(f, pic, out, out_pic, sem):
    a = pltpu.make_async_copy(f, out, sem.at[0])
    b = pltpu.make_async_copy(pic, out_pic, sem.at[1])
    a.start()
    b.start()
    a.wait()
    b.wait()


def solution(mesh):
    sizes = (mesh.shape["sx"], mesh.shape["sy"], mesh.shape["row"])
    n_row = sizes[2]

    def per_device(thermal_state, substance_label, thermal_coefficients, optical_thickness, substance_colours):
        depth, wide, tall = thermal_state.shape
        f32 = jnp.float32
        side = depth * wide // LANES
        near = pl.BlockSpec(memory_space=pltpu.VMEM)
        anywhere = pl.BlockSpec(memory_space=pl.ANY)
        chunks = depth // SUB
        results = (
            jax.ShapeDtypeStruct((depth, wide, tall), f32),
            jax.ShapeDtypeStruct((4, wide // n_row, tall), f32),
        )
        f, pic = pl.pallas_call(
            functools.partial(kernel, sizes),
            out_shape=results,
            in_specs=[anywhere] * 5,
            out_specs=(near, near),
            scratch_shapes=[
                pltpu.VMEM((depth + 2, wide, tall), f32),
                pltpu.VMEM((depth + 2, wide, tall), f32),
                pltpu.VMEM((depth + 2, wide, tall), f32),
                pltpu.VMEM((depth, wide, tall), f32),
                pltpu.VMEM((depth, wide, tall), f32),
                pltpu.VMEM((depth + 2, wide, tall), jnp.int32),
                pltpu.VMEM((2, 2, depth, tall), f32),
                pltpu.VMEM((2, 2, depth, tall), f32),
                pltpu.VMEM((2, depth, tall), f32),
                pltpu.VMEM((2, depth, tall), f32),
                pltpu.VMEM((2, 2 * SUB, tall), f32),
                pltpu.VMEM((2, 2 * SUB, tall), f32),
                pltpu.VMEM((2, depth + SUB, tall), f32),
                pltpu.VMEM((2, 3 * SUB, tall), f32),
                pltpu.VMEM((2, 2, side, tall), f32),
                pltpu.VMEM((2, 2, side, tall), f32),
                pltpu.VMEM((2, side, tall), f32),
                pltpu.VMEM((2, side, tall), f32),
                pltpu.VMEM((2, side, tall), f32),
                pltpu.VMEM((2, side, tall), f32),
                pltpu.VMEM((3, wide, tall), f32),
                pltpu.VMEM((n_row, 3, wide // n_row, tall), f32),
                pltpu.VMEM((n_row, 3, wide // n_row, tall), f32),
                pltpu.SMEM((3,), f32),
                pltpu.SMEM((3,), f32),
                pltpu.SMEM((3, 3), f32),
                pltpu.SemaphoreType.DMA((2, chunks)),
                pltpu.SemaphoreType.DMA((3,)),
                pltpu.SemaphoreType.DMA((2, 2, PARTS)),
                pltpu.SemaphoreType.DMA((2, 2, PARTS)),
                pltpu.SemaphoreType.DMA((2, PARTS)),
                pltpu.SemaphoreType.DMA((2, PARTS)),
                pltpu.SemaphoreType.DMA((12,)),
                pltpu.SemaphoreType.DMA((12,)),
                pltpu.SemaphoreType.DMA((n_row,)),
                pltpu.SemaphoreType.DMA((n_row,)),
            ],
            compiler_params=pltpu.CompilerParams(
                collective_id=0, has_side_effects=True, vmem_limit_bytes=VMEM_LIMIT
            ),
        )(*[
            pltpu.with_memory_space_constraint(a, pltpu.HBM)
            for a in (thermal_state, substance_label, thermal_coefficients, optical_thickness, substance_colours)
        ])
        return pl.pallas_call(
            deliver,
            out_shape=results,
            in_specs=[near, near],
            out_specs=(anywhere, anywhere),
            scratch_shapes=[pltpu.SemaphoreType.DMA((2,))],
            compiler_params=pltpu.CompilerParams(vmem_limit_bytes=VMEM_LIMIT),
        )(f, pic)

    placed = (P("row", "sx", "sy"), P("row", "sx", "sy"), P(), P(), P())
    return jax.shard_map(
        per_device,
        mesh=mesh,
        in_specs=placed,
        out_specs=(P("row", "sx", "sy"), P(None, ("sx", "row"), "sy")),
        check_vma=False,
    )
```

time: 26.9 us -> 27.1 us (level)
  the two profiles are of different devices: /device:TPU:64 before, /device:TPU:8 now
where the time goes in v3:
time: 27.1 us; the launch traced here: 27 us
  Pallas kernels  26.3 us (97%)
  between operations  0.64 us (2%)
    pallas_call x1, Pallas kernels, per_device(): pl.pallas_call(functools.partial(kernel, sizes), out_shape=results, in_sp...  25.4 us
    pallas_call x1, Pallas kernels, per_device(): pl.pallas_call(deliver, out_shape=results, in_specs=[near, near], out_spe...  0.99 us

profile of v3, /device:TPU:8, one launch (start us, length us, event | category | flops | bytes accessed | tf_op | source)
XLA Modules:
  0.0 27.0 jit_solution(17357838844553229926)
XLA Ops:
  0.6 25.4 %shard_map.68 = (f32[32,64,128]{2,1,0:T(8,128)S(1)}, f32[4,8,128]{2,1,0:T(8,128)S(1)}) custom-call(f32[32,64,128]{2,1,0:T(8,128)} %t_hbm.1, s32[32,64,128]{2,1,0:T(8,128)} %lab_hbm.1, f32[3]{0:T(128)} %coef_hbm.1, f32[3]{0:T(128)} %thick_hbm.1, f32[3,3]{1,0:T(4,128)} %tint_hbm.1), custom_call_target="tpu_custom_call" | custom-call | tf_op jit(solution)/shard_map/pallas_call | solution.py:490
  26.0 1.0 %shard_map.69 = (f32[32,64,128]{2,1,0:T(8,128)}, f32[4,8,128]{2,1,0:T(8,128)}) custom-call(f32[32,64,128]{2,1,0:T(8,128)S(1)} %get-tuple-element.4.f, f32[4,8,128]{2,1,0:T(8,128)S(1)} %get-tuple-element.5.pic), custom_call_target="tpu_custom_call" | custom-call | tf_op jit(solution)/shard_map/pallas_call | solution.py:540

commit v4 on v3

--- a/solution.py
+++ b/solution.py
@@ -9,7 +9,7 @@
 
 MESH = pl.DeviceIdType.MESH
 SUB, LANES = 8, 128
-FLUX, FIX, PACK, MARCH, PARTS = 4, 6, 6, 6, 4
+FLUX, PACK, MARCH, PARTS = 4, 4, 6, 4
 VMEM_LIMIT = 16 << 20
 
 
@@ -17,7 +17,7 @@
     sizes,
     t_hbm, lab_hbm, coef_hbm, thick_hbm, tint_hbm,
     f, pic_ref,
-    u, d, h, ky, fy, lab, xs, xr, xs2, xr2, xs3, xr3, fx, fx3, ys, yr, ys2, yr2, ys3, yr3, mid, ib, rb,
+    u, d, h, ky, fy, lab, xs, xr, xs2, xr2, fx, ys, yr, ys2, yr2, mid, ib, rb,
     coef, thick, tint, lsem, csem, zsem1, zrec1, zsem2, zrec2, ssem, rsem, asem, bsem,
 ):
     n_sx, n_sy, n_row = sizes
@@ -81,8 +81,8 @@
 
     clear(has_prev, (u.at[0], d.at[0], h.at[0]))
     clear(has_next, (u.at[depth + 1], d.at[depth + 1], h.at[depth + 1]))
-    clear(has_left, (yr.at[0], yr2.at[0], yr3.at[0]))
-    clear(has_right, (yr.at[1], yr2.at[1], yr3.at[1]))
+    clear(has_left, (yr.at[0], yr2.at[0]))
+    clear(has_right, (yr.at[1], yr2.at[1]))
 
     to_next, to_prev = {"row": me + 1}, {"row": me - 1}
     to_right, to_left = {"sy": my_sy + 1}, {"sy": my_sy - 1}
@@ -142,12 +142,6 @@
 
     y_first, x_first = y_copies(ys, yr, 0), x_copies(xs, xr, 2)
     y_second, x_second = y_copies(ys2, yr2, 4), x_copies(xs2, xr2, 6)
-    y_third, x_third = y_copies(ys3, yr3, 8), x_copies(xs3, xr3, 10)
-
-    waits = n_row + 1 + has_left.astype(jnp.int32) + has_right.astype(jnp.int32)
-    pl.semaphore_wait(barrier, waits)
-    for p in range(PARTS):
-        start(z_first(p))
 
     def rows(xb):
         return pl.ds(SUB * xb, SUB)
@@ -193,7 +187,6 @@
         at = pl.ds(SUB * g, SUB)
         ys[0, 0, at, :], ys[1, 0, at, :] = faces(au, g)
         ys[0, 1, at, :], ys[1, 1, at, :] = faces(ad, g)
-    start(y_first)
 
     def edge(ref, first, k, side):
         flat = ref.reshape(ref.shape[0] * wide, LANES)
@@ -207,6 +200,12 @@
         for k in range(chunks):
             for i, a in enumerate((u, d)):
                 xs[side, i, pl.ds(SUB * k, SUB), :] = edge(a, 1, k, side)
+
+    waits = n_row + 1 + has_left.astype(jnp.int32) + has_right.astype(jnp.int32)
+    pl.semaphore_wait(barrier, waits)
+    start(y_first)
+    for p in range(PARTS):
+        start(z_first(p))
     start(x_first)
 
     def flux(da, db, ub, ua):
@@ -262,13 +261,39 @@
         fz = plane(u, h, 0, z, fz, True, True)
     plane(u, h, 0, last, fz, False, True)
 
-    def x_faces(to, tiles, own, came):
+    def settle(dst, shift):
+        def some(j, carry):
+            for i in range(FLUX):
+                z0 = FLUX * j + i
+                for xb in range(blocks):
+                    dst[z0 + shift, rows(xb), :] = dst[z0 + shift, rows(xb), :] - pltpu.roll(fy[z0, rows(xb), :], 1, 1)
+            return carry
+
+        lax.fori_loop(0, depth // FLUX, some, 0)
+
+    def sweep(first, trips, count, body, carry):
+        def some(j, carry):
+            for i in range(count):
+                carry = body(count * j + first + i, carry, (first + i) % 2)
+            return carry
+
+        return lax.fori_loop(0, trips, some, carry)
+
+    settle(h, 1)
+
+    def pack_h(z0, acc, parity, which=range(blocks)):
+        acc = dict(acc)
+        for xb in which:
+            put(acc, h[z0 + 1, rows(xb), :], z0, parity, xb)
+        return acc
+
+    acc = dict(sweep(0, depth // PACK, PACK, pack_h, fresh()))
+
+    def x_faces(own, came):
         for side in (0, 1):
-            for i, k in enumerate(tiles):
-                at, place = pl.ds(SUB * k, SUB), pl.ds(SUB * i, SUB)
-                to[side, place, :] = flux(
-                    xs[side, 1, at, :], xr[side, 1, at, :], came(side, place), own(side, place)
-                )
+            for k in range(chunks):
+                at = pl.ds(SUB * k, SUB)
+                fx[side, at, :] = flux(xs[side, 1, at, :], xr[side, 1, at, :], came(side, at), own(side, at))
 
     def y_faces(own, came):
         even, odd = [], []
@@ -283,58 +308,22 @@
             odd.append(jnp.where(is_even, b, a))
         return even, odd
 
-    def with_faces(v, packed, rowsx, zx, z0, parity, xb):
+    def with_faces(v, packed, z0, parity, xb):
         r = pltpu.roll(packed[parity][xb // per_group], (LANES - spot(z0, xb)) & (LANES - 1), 1)
-        v = v - pltpu.roll(fy[z0, rows(xb), :], 1, 1)
         v = jnp.where(at_ends, v + r, v)
         if xb == 0:
-            v = jnp.where(sub == 0, v + rowsx[0, pl.ds(zx, SUB, stride=0), :], v)
+            v = jnp.where(sub == 0, v + fx[0, pl.ds(z0, SUB, stride=0), :], v)
         if xb == blocks - 1:
-            v = jnp.where(sub == SUB - 1, v + rowsx[1, pl.ds(zx, SUB, stride=0), :], v)
+            v = jnp.where(sub == SUB - 1, v + fx[1, pl.ds(z0, SUB, stride=0), :], v)
         return v
 
-    def sweep(count, body, carry):
-        def some(j, carry):
-            for i in range(count):
-                carry = body(count * j + 1 + i, (1 + i) % 2, carry)
-            return carry
-
-        return lax.fori_loop(0, (depth - 2) // count, some, carry)
-
     arrive(x_first)
-    x_faces(fx, range(chunks), lambda s, at: xs[s, 0, at, :], lambda s, at: xr[s, 0, at, :])
+    x_faces(lambda s, at: xs[s, 0, at, :], lambda s, at: xr[s, 0, at, :])
     arrive(y_first)
     packed = y_faces(lambda s, at: ys[s, 0, at, :], lambda s, at: yr[s, 0, at, :])
 
-    def fix_h(z0, parity, carry):
-        for xb in range(blocks):
-            h[z0 + 1, rows(xb), :] = with_faces(h[z0 + 1, rows(xb), :], packed, fx, z0, z0, parity, xb)
-        return carry
-
-    def pack_h(z0, parity, acc):
-        acc = dict(acc)
-        for xb in range(blocks):
-            put(acc, h[z0 + 1, rows(xb), :], z0, parity, xb)
-        return acc
-
-    sweep(FIX, fix_h, 0)
-    acc = dict(sweep(PACK, pack_h, fresh()))
-
-    def y_out(to, acc):
-        for g in range(groups):
-            at = pl.ds(SUB * g, SUB)
-            to[0, at, :], to[1, at, :] = faces(acc, g)
-
-    y_out(ys2, acc)
-    start(y_second)
-    for side in (0, 1):
-        for k in range(chunks):
-            xs2[side, pl.ds(SUB * k, SUB), :] = edge(h, 1, k, side)
-    start(x_second)
-    planes(h, f, -1, 3, depth - 4, between(h, 2), False)
-
     outer = ((0, 0, 0), (depth - 1, depth + 1, 1))
-    tiles = (0, chunks - 1)
+    brims = (0, blocks - 1)
 
     for p in range(PARTS):
         arrive(z_first(p))
@@ -344,34 +333,40 @@
                 dg = jnp.where(inside, conduct(lab[ghost, at, :]), 0.0)
                 d[ghost, at, :] = dg
                 fz = flux(d[z0 + 1, at, :], dg, u[ghost, at, :], u[z0 + 1, at, :])
-                h[z0 + 1, at, :] = with_faces(h[z0 + 1, at, :] + fz, packed, fx, z0, z0, parity, xb)
+                h[z0 + 1, at, :] = with_faces(h[z0 + 1, at, :] + fz, packed, z0, parity, xb)
         start(z_second(p))
 
+    def fix_h(which):
+        def body(z0, carry, parity):
+            for xb in which:
+                h[z0 + 1, rows(xb), :] = with_faces(h[z0 + 1, rows(xb), :], packed, z0, parity, xb)
+            return carry
+
+        return body
+
+    sweep(1, 3, 10, fix_h(brims), 0)
+    for p in (0, 1):
+        for g in range(groups):
+            acc[p, g] = acc[p, g] + packed[p][g]
     for z0, _, parity in outer:
-        acc = pack_h(z0, parity, acc)
-    y_out(ys3, acc)
-    start(y_third)
+        acc = pack_h(z0, acc, parity)
+    acc = dict(sweep(1, 3, 10, functools.partial(pack_h, which=brims), acc))
+    for g in range(groups):
+        at = pl.ds(SUB * g, SUB)
+        ys2[0, at, :], ys2[1, at, :] = faces(acc, g)
+    start(y_second)
     for side in (0, 1):
-        for i, k in enumerate(tiles):
-            xs3[side, pl.ds(SUB * i, SUB), :] = edge(h, 1, k, side)
-    start(x_third)
+        for k in range(chunks):
+            xs2[side, pl.ds(SUB * k, SUB), :] = edge(h, 1, k, side)
+    start(x_second)
+    sweep(1, 5, 6, fix_h(range(1, blocks - 1)), 0)
 
     fz = plane(h, f, -1, 1, None, True, False)
-    plane(h, f, -1, 2, fz, True, False)
-    fz = plane(h, f, -1, last - 1, between(h, last - 2), True, False)
+    fz = planes(h, f, -1, 2, depth - FLUX, fz, False)
+    for z in range(depth - FLUX + 2, last):
+        fz = plane(h, f, -1, z, fz, True, False)
     plane(h, f, -1, last, fz, False, False)
-
-    arrive(x_second)
-    x_faces(fx, range(chunks), lambda s, at: xs2[s, at, :], lambda s, at: xr2[s, at, :])
-    arrive(y_second)
-    packed2 = y_faces(lambda s, at: ys2[s, at, :], lambda s, at: yr2[s, at, :])
-
-    def fix_f(z0, parity, carry):
-        for xb in range(blocks):
-            f[z0, rows(xb), :] = with_faces(f[z0, rows(xb), :], packed2, fx, z0, z0, parity, xb)
-        return carry
-
-    sweep(FIX, fix_f, 0)
+    settle(f, 0)
 
     load_k.wait()
     scale = 0.5 / (depth * n_row)
@@ -382,30 +377,30 @@
         half = jnp.where(first, k0, jnp.where(second, k1, k2))
         return half + half * jnp.tanh(0.5 * v), first, second
 
-    def march(z0, parity, carry):
+    arrive(x_second)
+    x_faces(lambda s, at: xs2[s, at, :], lambda s, at: xr2[s, at, :])
+    arrive(y_second)
+    packed2 = y_faces(lambda s, at: ys2[s, at, :], lambda s, at: yr2[s, at, :])
+
+    def march(z0, carry, parity):
         through, w0, w1 = [list(c) for c in carry]
         for xb in range(blocks):
-            a, first, second = opaque(f[z0, rows(xb), :], lab[z0 + 1, rows(xb), :])
+            v = with_faces(f[z0, rows(xb), :], packed2, z0, parity, xb)
+            f[z0, rows(xb), :] = v
+            a, first, second = opaque(v, lab[z0 + 1, rows(xb), :])
             w = through[xb] * a
             through[xb] = through[xb] - w
             w0[xb] = w0[xb] + jnp.where(first, w, 0.0)
             w1[xb] = w1[xb] + jnp.where(second, w, 0.0)
         return tuple(tuple(c) for c in (through, w0, w1))
 
-    state = sweep(MARCH, march, ((one,) * blocks,) + ((zero,) * blocks,) * 2)
+    state = sweep(1, (depth - 2) // MARCH, MARCH, march, ((one,) * blocks,) + ((zero,) * blocks,) * 2)
     for i in range(3):
         for xb in range(blocks):
             mid[i, rows(xb), :] = state[i][xb]
-
-    arrive(x_third)
-    x_faces(fx3, tiles, lambda s, at: xs3[s, at, :], lambda s, at: xr3[s, at, :])
-    arrive(y_third)
-    packed3 = y_faces(lambda s, at: ys3[s, at, :], lambda s, at: yr3[s, at, :])
     for z0, _, parity in outer:
         for xb in range(blocks):
-            f[z0, rows(xb), :] = with_faces(
-                f[z0, rows(xb), :], packed3, fx3, z0 if z0 == 0 else 2 * SUB - 1, z0, parity, xb
-            )
+            f[z0, rows(xb), :] = with_faces(f[z0, rows(xb), :], packed2, z0, parity, xb)
     load_p.wait()
 
     def hand(dest):
@@ -459,7 +454,7 @@
     for p in range(PARTS):
         left_here(z_first(p))
         left_here(z_second(p))
-    for copies in (y_first, x_first, y_second, x_second, y_third, x_third):
+    for copies in (y_first, x_first, y_second, x_second):
         left_here(copies)
 
 
@@ -503,14 +498,9 @@
                 pltpu.VMEM((2, 2, depth, tall), f32),
                 pltpu.VMEM((2, depth, tall), f32),
                 pltpu.VMEM((2, depth, tall), f32),
-                pltpu.VMEM((2, 2 * SUB, tall), f32),
-                pltpu.VMEM((2, 2 * SUB, tall), f32),
                 pltpu.VMEM((2, depth + SUB, tall), f32),
-                pltpu.VMEM((2, 3 * SUB, tall), f32),
                 pltpu.VMEM((2, 2, side, tall), f32),
                 pltpu.VMEM((2, 2, side, tall), f32),
-                pltpu.VMEM((2, side, tall), f32),
-                pltpu.VMEM((2, side, tall), f32),
                 pltpu.VMEM((2, side, tall), f32),
                 pltpu.VMEM((2, side, tall), f32),
                 pltpu.VMEM((3, wide, tall), f32),
@@ -525,8 +515,8 @@
                 pltpu.SemaphoreType.DMA((2, 2, PARTS)),
                 pltpu.SemaphoreType.DMA((2, PARTS)),
                 pltpu.SemaphoreType.DMA((2, PARTS)),
-                pltpu.SemaphoreType.DMA((12,)),
-                pltpu.SemaphoreType.DMA((12,)),
+                pltpu.SemaphoreType.DMA((8,)),
+                pltpu.SemaphoreType.DMA((8,)),
                 pltpu.SemaphoreType.DMA((n_row,)),
                 pltpu.SemaphoreType.DMA((n_row,)),
             ],

time: 27.1 us -> 24.6 us (0.908)
  the two profiles are of different devices: /device:TPU:8 before, /device:TPU:24 now
where the time goes in v4:
time: 24.6 us; the launch traced here: 24.5 us
  Pallas kernels  23.8 us (97%)
  between operations  0.64 us (3%)
    pallas_call x1, Pallas kernels, per_device(): pl.pallas_call(functools.partial(kernel, sizes), out_shape=results, in_sp...  22.9 us
    pallas_call x1, Pallas kernels, per_device(): pl.pallas_call(deliver, out_shape=results, in_specs=[near, near], out_spe...  0.99 us

profile of v4, /device:TPU:24, one launch (start us, length us, event | category | flops | bytes accessed | tf_op | source)
XLA Modules:
  0.0 24.5 jit_solution(13812398601898392332)
XLA Ops:
  0.6 22.9 %shard_map.68 = (f32[32,64,128]{2,1,0:T(8,128)S(1)}, f32[4,8,128]{2,1,0:T(8,128)S(1)}) custom-call(f32[32,64,128]{2,1,0:T(8,128)} %t_hbm.1, s32[32,64,128]{2,1,0:T(8,128)} %lab_hbm.1, f32[3]{0:T(128)} %coef_hbm.1, f32[3]{0:T(128)} %thick_hbm.1, f32[3,3]{1,0:T(4,128)} %tint_hbm.1), custom_call_target="tpu_custom_call" | custom-call | tf_op jit(solution)/shard_map/pallas_call | solution.py:485
  23.5 1.0 %shard_map.69 = (f32[32,64,128]{2,1,0:T(8,128)}, f32[4,8,128]{2,1,0:T(8,128)}) custom-call(f32[32,64,128]{2,1,0:T(8,128)S(1)} %get-tuple-element.4.f, f32[4,8,128]{2,1,0:T(8,128)S(1)} %get-tuple-element.5.pic), custom_call_target="tpu_custom_call" | custom-call | tf_op jit(solution)/shard_map/pallas_call | solution.py:530

commit v5 on v4

--- a/solution.py
+++ b/solution.py
@@ -18,7 +18,7 @@
     t_hbm, lab_hbm, coef_hbm, thick_hbm, tint_hbm,
     f, pic_ref,
     u, d, h, ky, fy, lab, xs, xr, xs2, xr2, fx, ys, yr, ys2, yr2, mid, ib, rb,
-    coef, thick, tint, lsem, csem, zsem1, zrec1, zsem2, zrec2, ssem, rsem, asem, bsem,
+    coef, thick, tint, lsem, csem, zsem1, zrec1, zsem2, zrec2, ssem, rsem, asem, bsem, hello,
 ):
     n_sx, n_sy, n_row = sizes
     depth, wide = t_hbm.shape[0], t_hbm.shape[1]
@@ -49,21 +49,25 @@
     load_k.start()
     load_p.start()
 
-    barrier = pltpu.get_barrier_semaphore()
-    for o in range(1, n_row):
-        pl.semaphore_signal(barrier, inc=1, device_id={"row": lax.rem(me + o, n_row)}, device_id_type=MESH)
     sx_next = lax.rem(my_sx + 1, n_sx)
     sx_prev = lax.rem(my_sx + n_sx - 1, n_sx)
-    pl.semaphore_signal(barrier, inc=1, device_id={"sx": sx_next}, device_id_type=MESH)
-    pl.semaphore_signal(barrier, inc=1, device_id={"sx": sx_prev}, device_id_type=MESH)
-
-    @pl.when(has_left)
-    def _():
-        pl.semaphore_signal(barrier, inc=1, device_id={"sy": my_sy - 1}, device_id_type=MESH)
-
-    @pl.when(has_right)
-    def _():
-        pl.semaphore_signal(barrier, inc=1, device_id={"sy": my_sy + 1}, device_id_type=MESH)
+    to_next, to_prev = {"row": me + 1}, {"row": me - 1}
+    to_right, to_left = {"sy": my_sy + 1}, {"sy": my_sy - 1}
+    to_up, to_down = {"sx": sx_next}, {"sx": sx_prev}
+
+    def only(cond, act):
+        if cond is None:
+            act()
+        else:
+            pl.when(cond)(act)
+
+    barrier = pltpu.get_barrier_semaphore()
+    near = (
+        (has_prev, to_prev), (has_next, to_next), (has_left, to_left), (has_right, to_right),
+        (None, to_up), (None, to_down),
+    )
+    for there, where in near:
+        only(there, functools.partial(pl.semaphore_signal, barrier, inc=1, device_id=where, device_id_type=MESH))
 
     lane = lax.broadcasted_iota(jnp.int32, (SUB, LANES), 1)
     sub = lax.broadcasted_iota(jnp.int32, (SUB, LANES), 0)
@@ -83,16 +87,6 @@
     clear(has_next, (u.at[depth + 1], d.at[depth + 1], h.at[depth + 1]))
     clear(has_left, (yr.at[0], yr2.at[0]))
     clear(has_right, (yr.at[1], yr2.at[1]))
-
-    to_next, to_prev = {"row": me + 1}, {"row": me - 1}
-    to_right, to_left = {"sy": my_sy + 1}, {"sy": my_sy - 1}
-    to_up, to_down = {"sx": sx_next}, {"sx": sx_prev}
-
-    def only(cond, act):
-        if cond is None:
-            act()
-        else:
-            pl.when(cond)(act)
 
     def start(copies):
         for copy, sends, _ in copies:
@@ -142,6 +136,19 @@
 
     y_first, x_first = y_copies(ys, yr, 0), x_copies(xs, xr, 2)
     y_second, x_second = y_copies(ys2, yr2, 4), x_copies(xs2, xr2, 6)
+
+    pl.semaphore_wait(barrier, 2 + sum(c.astype(jnp.int32) for c in (has_prev, has_next, has_left, has_right)))
+    for p in range(PARTS):
+        start(z_first(p))
+
+    def greet(i, apart, act):
+        for side, there, where in ((0, me >= apart, me - apart), (1, me + apart < n_row, me + apart)):
+            @pl.when(there)
+            def _():
+                if act == "signal":
+                    pl.semaphore_signal(hello.at[i, 1 - side], inc=1, device_id={"row": where}, device_id_type=MESH)
+                else:
+                    pl.semaphore_wait(hello.at[i, side], 1)
 
     def rows(xb):
         return pl.ds(SUB * xb, SUB)
@@ -187,6 +194,7 @@
         at = pl.ds(SUB * g, SUB)
         ys[0, 0, at, :], ys[1, 0, at, :] = faces(au, g)
         ys[0, 1, at, :], ys[1, 1, at, :] = faces(ad, g)
+    start(y_first)
 
     def edge(ref, first, k, side):
         flat = ref.reshape(ref.shape[0] * wide, LANES)
@@ -201,11 +209,6 @@
             for i, a in enumerate((u, d)):
                 xs[side, i, pl.ds(SUB * k, SUB), :] = edge(a, 1, k, side)
 
-    waits = n_row + 1 + has_left.astype(jnp.int32) + has_right.astype(jnp.int32)
-    pl.semaphore_wait(barrier, waits)
-    start(y_first)
-    for p in range(PARTS):
-        start(z_first(p))
     start(x_first)
 
     def flux(da, db, ub, ua):
@@ -335,6 +338,7 @@
                 fz = flux(d[z0 + 1, at, :], dg, u[ghost, at, :], u[z0 + 1, at, :])
                 h[z0 + 1, at, :] = with_faces(h[z0 + 1, at, :] + fz, packed, z0, parity, xb)
         start(z_second(p))
+    greet(0, 2, "signal")
 
     def fix_h(which):
         def body(z0, carry, parity):
@@ -360,6 +364,8 @@
             xs2[side, pl.ds(SUB * k, SUB), :] = edge(h, 1, k, side)
     start(x_second)
     sweep(1, 5, 6, fix_h(range(1, blocks - 1)), 0)
+    greet(0, 2, "wait")
+    greet(1, 4, "signal")
 
     fz = plane(h, f, -1, 1, None, True, False)
     fz = planes(h, f, -1, 2, depth - FLUX, fz, False)
@@ -403,38 +409,43 @@
             f[z0, rows(xb), :] = with_faces(f[z0, rows(xb), :], packed2, z0, parity, xb)
     load_p.wait()
 
-    def hand(dest):
+    for p in range(PARTS):
+        arrive(z_second(p))
+    for xb in range(blocks):
+        at = rows(xb)
+        ends = []
+        for z0, ghost, parity in outer:
+            fz = flux(d[z0 + 1, at, :], d[ghost, at, :], h[ghost, at, :], h[z0 + 1, at, :])
+            v = f[z0, at, :] + fz
+            f[z0, at, :] = v
+            ends.append(opaque(v, lab[z0 + 1, at, :]))
+        (a, fa, fb), (b, ga, gb) = ends
+        clear_a = 1.0 - a
+        through = clear_a * mid[0, at, :]
+        w = through * b
+        ib[xb, 0] = jnp.where(fa, a, 0.0) + clear_a * mid[1, at, :] + jnp.where(ga, w, 0.0)
+        ib[xb, 1] = jnp.where(fb, a, 0.0) + clear_a * mid[2, at, :] + jnp.where(gb, w, 0.0)
+        ib[xb, 2] = through - w
+
+    def hand(o):
+        dest = lax.rem(me + o, n_row)
         return pltpu.make_async_remote_copy(
-            src_ref=ib.at[dest], dst_ref=rb.at[me], send_sem=asem.at[dest], recv_sem=bsem.at[me],
+            src_ref=ib.at[dest], dst_ref=rb.at[me], send_sem=asem.at[o], recv_sem=bsem.at[me],
             device_id={"row": dest}, device_id_type=MESH,
         )
 
-    for p in range(PARTS):
-        arrive(z_second(p))
-        for xb in range(per_part * p, per_part * (p + 1)):
-            at = rows(xb)
-            ends = []
-            for z0, ghost, parity in outer:
-                fz = flux(d[z0 + 1, at, :], d[ghost, at, :], h[ghost, at, :], h[z0 + 1, at, :])
-                v = f[z0, at, :] + fz
-                f[z0, at, :] = v
-                ends.append(opaque(v, lab[z0 + 1, at, :]))
-            (a, fa, fb), (b, ga, gb) = ends
-            clear_a = 1.0 - a
-            through = clear_a * mid[0, at, :]
-            w = through * b
-            ib[xb, 0] = jnp.where(fa, a, 0.0) + clear_a * mid[1, at, :] + jnp.where(ga, w, 0.0)
-            ib[xb, 1] = jnp.where(fb, a, 0.0) + clear_a * mid[2, at, :] + jnp.where(gb, w, 0.0)
-            ib[xb, 2] = through - w
-        for dest in range(per_part * p, per_part * (p + 1)):
-            pl.when(me != dest)(hand(dest).start)
+    greet(1, 4, "wait")
+    half = n_row // 2
+    order = sorted(range(1, n_row), key=lambda o: abs(o - half))
+    for o in order:
+        hand(o).start()
     rb[me] = ib[me]
 
     for s in range(n_row):
         @pl.when(me != s)
         def _():
             pltpu.make_async_remote_copy(
-                src_ref=ib.at[s], dst_ref=rb.at[s], send_sem=asem.at[s], recv_sem=bsem.at[s],
+                src_ref=ib.at[s], dst_ref=rb.at[s], send_sem=asem.at[0], recv_sem=bsem.at[s],
                 device_id={"row": s}, device_id_type=MESH,
             ).wait_recv()
 
@@ -449,8 +460,8 @@
         pic_ref[c] = w0 * tint[0, c] + w1 * tint[1, c] + w2 * tint[2, c]
     pic_ref[3] = blocked
 
-    for dest in range(n_row):
-        pl.when(me != dest)(hand(dest).wait_send)
+    for o in order:
+        hand(o).wait_send()
     for p in range(PARTS):
         left_here(z_first(p))
         left_here(z_second(p))
@@ -519,6 +530,7 @@
                 pltpu.SemaphoreType.DMA((8,)),
                 pltpu.SemaphoreType.DMA((n_row,)),
                 pltpu.SemaphoreType.DMA((n_row,)),
+                pltpu.SemaphoreType.REGULAR((2, 2)),
             ],
             compiler_params=pltpu.CompilerParams(
                 collective_id=0, has_side_effects=True, vmem_limit_bytes=VMEM_LIMIT

time: 24.6 us -> 25.8 us (1.049)
  the two profiles are of different devices: /device:TPU:24 before, /device:TPU:8 now
where the time goes in v5:
time: 25.8 us; the launch traced here: 25.7 us
  Pallas kernels  25.1 us (97%)
  between operations  0.64 us (2%)
    pallas_call x1, Pallas kernels, per_device(): pl.pallas_call(functools.partial(kernel, sizes), out_shape=results, in_sp...  24.1 us
    pallas_call x1, Pallas kernels, per_device(): pl.pallas_call(deliver, out_shape=results, in_specs=[near, near], out_spe...  0.99 us

profile of v5, /device:TPU:8, one launch (start us, length us, event | category | flops | bytes accessed | tf_op | source)
XLA Modules:
  0.0 25.7 jit_solution(686151613494027063)
XLA Ops:
  0.6 24.1 %shard_map.68 = (f32[32,64,128]{2,1,0:T(8,128)S(1)}, f32[4,8,128]{2,1,0:T(8,128)S(1)}) custom-call(f32[32,64,128]{2,1,0:T(8,128)} %t_hbm.1, s32[32,64,128]{2,1,0:T(8,128)} %lab_hbm.1, f32[3]{0:T(128)} %coef_hbm.1, f32[3]{0:T(128)} %thick_hbm.1, f32[3,3]{1,0:T(4,128)} %tint_hbm.1), custom_call_target="tpu_custom_call" | custom-call | tf_op jit(solution)/shard_map/pallas_call | solution.py:496
  24.7 1.0 %shard_map.69 = (f32[32,64,128]{2,1,0:T(8,128)}, f32[4,8,128]{2,1,0:T(8,128)}) custom-call(f32[32,64,128]{2,1,0:T(8,128)S(1)} %get-tuple-element.4.f, f32[4,8,128]{2,1,0:T(8,128)S(1)} %get-tuple-element.5.pic), custom_call_target="tpu_custom_call" | custom-call | tf_op jit(solution)/shard_map/pallas_call | solution.py:542

commit v6 on v5

--- a/solution.py
+++ b/solution.py
@@ -9,7 +9,7 @@
 
 MESH = pl.DeviceIdType.MESH
 SUB, LANES = 8, 128
-FLUX, PACK, MARCH, PARTS = 4, 4, 6, 4
+FLUX, PACK, MARCH, PARTS = 4, 4, 6, 2
 VMEM_LIMIT = 16 << 20
 
 
@@ -18,7 +18,7 @@
     t_hbm, lab_hbm, coef_hbm, thick_hbm, tint_hbm,
     f, pic_ref,
     u, d, h, ky, fy, lab, xs, xr, xs2, xr2, fx, ys, yr, ys2, yr2, mid, ib, rb,
-    coef, thick, tint, lsem, csem, zsem1, zrec1, zsem2, zrec2, ssem, rsem, asem, bsem, hello,
+    coef, thick, tint, lsem, csem, zsem1, zrec1, zsem2, zrec2, ssem, rsem, asem, bsem, hello, above,
 ):
     n_sx, n_sy, n_row = sizes
     depth, wide = t_hbm.shape[0], t_hbm.shape[1]
@@ -63,8 +63,7 @@
 
     barrier = pltpu.get_barrier_semaphore()
     near = (
-        (has_prev, to_prev), (has_next, to_next), (has_left, to_left), (has_right, to_right),
-        (None, to_up), (None, to_down),
+        (has_prev, to_prev), (has_next, to_next), (has_right, to_right), (None, to_up), (None, to_down),
     )
     for there, where in near:
         only(there, functools.partial(pl.semaphore_signal, barrier, inc=1, device_id=where, device_id_type=MESH))
@@ -123,10 +122,10 @@
         ]
 
     def y_copies(src, dst, s):
-        return [
-            (remote(src.at[1], dst.at[0], ssem.at[s], rsem.at[s], to_right), has_right, has_left),
-            (remote(src.at[0], dst.at[1], ssem.at[s + 1], rsem.at[s + 1], to_left), has_left, has_right),
-        ]
+        return (
+            [(remote(src.at[0], dst.at[1], ssem.at[s + 1], rsem.at[s + 1], to_left), has_left, has_right)],
+            [(remote(src.at[1], dst.at[0], ssem.at[s], rsem.at[s], to_right), has_right, has_left)],
+        )
 
     def x_copies(src, dst, s):
         return [
@@ -134,12 +133,13 @@
             (remote(src.at[0], dst.at[1], ssem.at[s + 1], rsem.at[s + 1], to_down), None, None),
         ]
 
-    y_first, x_first = y_copies(ys, yr, 0), x_copies(xs, xr, 2)
-    y_second, x_second = y_copies(ys2, yr2, 4), x_copies(xs2, xr2, 6)
-
-    pl.semaphore_wait(barrier, 2 + sum(c.astype(jnp.int32) for c in (has_prev, has_next, has_left, has_right)))
-    for p in range(PARTS):
-        start(z_first(p))
+    (y_down, y_up), x_first = y_copies(ys, yr, 0), x_copies(xs, xr, 2)
+    (y_down2, y_up2), x_second = y_copies(ys2, yr2, 4), x_copies(xs2, xr2, 6)
+
+    pl.semaphore_wait(barrier, 2 + sum(c.astype(jnp.int32) for c in (has_prev, has_next, has_left)))
+    only(has_left, functools.partial(pl.semaphore_signal, above, inc=1, device_id=to_left, device_id_type=MESH))
+    waits_long = has_right & (my_sy == n_sy // 2 - 1)
+    waits_short = has_right & (my_sy != n_sy // 2 - 1)
 
     def greet(i, apart, act):
         for side, there, where in ((0, me >= apart, me - apart), (1, me + apart < n_row, me + apart)):
@@ -194,7 +194,16 @@
         at = pl.ds(SUB * g, SUB)
         ys[0, 0, at, :], ys[1, 0, at, :] = faces(au, g)
         ys[0, 1, at, :], ys[1, 1, at, :] = faces(ad, g)
-    start(y_first)
+    start(y_down)
+
+    def meet_above(cond):
+        @pl.when(cond)
+        def _():
+            pl.semaphore_wait(above, 1)
+            for copy, _, _ in y_up:
+                copy.start()
+
+    meet_above(waits_short)
 
     def edge(ref, first, k, side):
         flat = ref.reshape(ref.shape[0] * wide, LANES)
@@ -210,6 +219,8 @@
                 xs[side, i, pl.ds(SUB * k, SUB), :] = edge(a, 1, k, side)
 
     start(x_first)
+    for p in range(PARTS):
+        start(z_first(p))
 
     def flux(da, db, ub, ua):
         return (da + db) * (ub - ua)
@@ -291,6 +302,7 @@
         return acc
 
     acc = dict(sweep(0, depth // PACK, PACK, pack_h, fresh()))
+    meet_above(waits_long)
 
     def x_faces(own, came):
         for side in (0, 1):
@@ -298,18 +310,22 @@
                 at = pl.ds(SUB * k, SUB)
                 fx[side, at, :] = flux(xs[side, 1, at, :], xr[side, 1, at, :], came(side, at), own(side, at))
 
-    def y_faces(own, came):
-        even, odd = [], []
+    def y_faces(own, came, with_high=True):
+        even, odd, highs = [], [], []
         for g in range(groups):
             at = pl.ds(SUB * g, SUB)
             dl, dr, ul, ur = ys[0, 1, at, :], ys[1, 1, at, :], own(0, at), own(1, at)
             closed = flux(dl, dr, ul, ur)
             a = flux(dl, yr[0, 1, at, :], came(0, at), ul) + closed
-            b = flux(dr, yr[1, 1, at, :], came(1, at), ur) - closed
+            b = zero - closed
+            if with_high:
+                high = flux(dr, yr[1, 1, at, :], came(1, at), ur)
+                highs.append(high)
+                b = b + high
             b = pltpu.roll(b, LANES - 1, 1)
             even.append(jnp.where(is_even, a, b))
             odd.append(jnp.where(is_even, b, a))
-        return even, odd
+        return (even, odd), highs
 
     def with_faces(v, packed, z0, parity, xb):
         r = pltpu.roll(packed[parity][xb // per_group], (LANES - spot(z0, xb)) & (LANES - 1), 1)
@@ -320,25 +336,46 @@
             v = jnp.where(sub == SUB - 1, v + fx[1, pl.ds(z0, SUB, stride=0), :], v)
         return v
 
+    own_y, came_y = lambda s, at: ys[s, 0, at, :], lambda s, at: yr[s, 0, at, :]
     arrive(x_first)
     x_faces(lambda s, at: xs[s, 0, at, :], lambda s, at: xr[s, 0, at, :])
-    arrive(y_first)
-    packed = y_faces(lambda s, at: ys[s, 0, at, :], lambda s, at: yr[s, 0, at, :])
+    arrive(y_up)
+    packed, _ = y_faces(own_y, came_y, with_high=False)
 
     outer = ((0, 0, 0), (depth - 1, depth + 1, 1))
     brims = (0, blocks - 1)
 
+    for p in (0, 1):
+        for g in range(groups):
+            acc[p, g] = acc[p, g] + packed[p][g]
+
+    def pack_brims(z0, acc, parity):
+        acc = dict(acc)
+        for xb in brims:
+            put(acc, with_faces(h[z0 + 1, rows(xb), :], packed, z0, parity, xb), z0, parity, xb)
+        return acc
+
+    acc = dict(sweep(1, 3, 10, pack_brims, acc))
     for p in range(PARTS):
         arrive(z_first(p))
-        for (z0, ghost, parity), inside in zip(outer, (has_prev, has_next)):
-            for xb in range(per_part * p, per_part * (p + 1)):
-                at = rows(xb)
-                dg = jnp.where(inside, conduct(lab[ghost, at, :]), 0.0)
-                d[ghost, at, :] = dg
-                fz = flux(d[z0 + 1, at, :], dg, u[ghost, at, :], u[z0 + 1, at, :])
-                h[z0 + 1, at, :] = with_faces(h[z0 + 1, at, :] + fz, packed, z0, parity, xb)
-        start(z_second(p))
-    greet(0, 2, "signal")
+    for (z0, ghost, parity), inside in zip(outer, (has_prev, has_next)):
+        for xb in range(blocks):
+            at = rows(xb)
+            dg = jnp.where(inside, conduct(lab[ghost, at, :]), 0.0)
+            d[ghost, at, :] = dg
+            v = h[z0 + 1, at, :] + flux(d[z0 + 1, at, :], dg, u[ghost, at, :], u[z0 + 1, at, :])
+            h[z0 + 1, at, :] = v
+            put(acc, with_faces(v, packed, z0, parity, xb), z0, parity, xb)
+    ends = [faces(acc, g) for g in range(groups)]
+    for g in range(groups):
+        ys2[0, pl.ds(SUB * g, SUB), :] = ends[g][0]
+    start(y_down2)
+
+    arrive(y_down)
+    packed, highs = y_faces(own_y, came_y)
+    for g in range(groups):
+        ys2[1, pl.ds(SUB * g, SUB), :] = ends[g][1] + highs[g]
+    start(y_up2)
 
     def fix_h(which):
         def body(z0, carry, parity):
@@ -348,17 +385,12 @@
 
         return body
 
+    for z0, _, parity in outer:
+        fix_h(range(blocks))(z0, 0, parity)
+    for p in range(PARTS):
+        start(z_second(p))
+    greet(0, 2, "signal")
     sweep(1, 3, 10, fix_h(brims), 0)
-    for p in (0, 1):
-        for g in range(groups):
-            acc[p, g] = acc[p, g] + packed[p][g]
-    for z0, _, parity in outer:
-        acc = pack_h(z0, acc, parity)
-    acc = dict(sweep(1, 3, 10, functools.partial(pack_h, which=brims), acc))
-    for g in range(groups):
-        at = pl.ds(SUB * g, SUB)
-        ys2[0, at, :], ys2[1, at, :] = faces(acc, g)
-    start(y_second)
     for side in (0, 1):
         for k in range(chunks):
             xs2[side, pl.ds(SUB * k, SUB), :] = edge(h, 1, k, side)
@@ -385,8 +417,9 @@
 
     arrive(x_second)
     x_faces(lambda s, at: xs2[s, at, :], lambda s, at: xr2[s, at, :])
-    arrive(y_second)
-    packed2 = y_faces(lambda s, at: ys2[s, at, :], lambda s, at: yr2[s, at, :])
+    arrive(y_up2)
+    arrive(y_down2)
+    packed2, _ = y_faces(lambda s, at: ys2[s, at, :], lambda s, at: yr2[s, at, :])
 
     def march(z0, carry, parity):
         through, w0, w1 = [list(c) for c in carry]
@@ -465,7 +498,7 @@
     for p in range(PARTS):
         left_here(z_first(p))
         left_here(z_second(p))
-    for copies in (y_first, x_first, y_second, x_second):
+    for copies in (y_down, y_up, x_first, y_down2, y_up2, x_second):
         left_here(copies)
 
 
@@ -531,6 +564,7 @@
                 pltpu.SemaphoreType.DMA((n_row,)),
                 pltpu.SemaphoreType.DMA((n_row,)),
                 pltpu.SemaphoreType.REGULAR((2, 2)),
+                pltpu.SemaphoreType.REGULAR,
             ],
             compiler_params=pltpu.CompilerParams(
                 collective_id=0, has_side_effects=True, vmem_limit_bytes=VMEM_LIMIT

time: 25.8 us -> 24.5 us (0.950)
  the two profiles are of different devices: /device:TPU:8 before, /device:TPU:64 now
where the time goes in v6:
time: 24.5 us; the launch traced here: 24.4 us
  Pallas kernels  23.8 us (97%)
  between operations  0.64 us (3%)
    pallas_call x1, Pallas kernels, per_device(): pl.pallas_call(functools.partial(kernel, sizes), out_shape=results, in_sp...  22.8 us
    pallas_call x1, Pallas kernels, per_device(): pl.pallas_call(deliver, out_shape=results, in_specs=[near, near], out_spe...  0.99 us

profile of v6, /device:TPU:64, one launch (start us, length us, event | category | flops | bytes accessed | tf_op | source)
XLA Modules:
  0.0 24.4 jit_solution(10219133764243908088)
XLA Ops:
  0.6 22.8 %shard_map.68 = (f32[32,64,128]{2,1,0:T(8,128)S(1)}, f32[4,8,128]{2,1,0:T(8,128)S(1)}) custom-call(f32[32,64,128]{2,1,0:T(8,128)} %t_hbm.1, s32[32,64,128]{2,1,0:T(8,128)} %lab_hbm.1, f32[3]{0:T(128)} %coef_hbm.1, f32[3]{0:T(128)} %thick_hbm.1, f32[3,3]{1,0:T(4,128)} %tint_hbm.1), custom_call_target="tpu_custom_call" | custom-call | tf_op jit(solution)/shard_map/pallas_call | solution.py:529
  23.4 1.0 %shard_map.69 = (f32[32,64,128]{2,1,0:T(8,128)}, f32[4,8,128]{2,1,0:T(8,128)}) custom-call(f32[32,64,128]{2,1,0:T(8,128)S(1)} %get-tuple-element.4.f, f32[4,8,128]{2,1,0:T(8,128)S(1)} %get-tuple-element.5.pic), custom_call_target="tpu_custom_call" | custom-call | tf_op jit(solution)/shard_map/pallas_call | solution.py:576

commit v7 on v6

--- a/solution.py
+++ b/solution.py
@@ -9,7 +9,7 @@
 
 MESH = pl.DeviceIdType.MESH
 SUB, LANES = 8, 128
-FLUX, PACK, MARCH, PARTS = 4, 4, 6, 2
+FLUX, PACK, MARCH, PARTS = 4, 4, 4, 1
 VMEM_LIMIT = 16 << 20
 
 
@@ -17,7 +17,7 @@
     sizes,
     t_hbm, lab_hbm, coef_hbm, thick_hbm, tint_hbm,
     f, pic_ref,
-    u, d, h, ky, fy, lab, xs, xr, xs2, xr2, fx, ys, yr, ys2, yr2, mid, ib, rb,
+    u, d, h, ky, fy, lab, xs, xr, xs2, xr2, fx, ys, yr, ys2, yr2, turn, ib, rb,
     coef, thick, tint, lsem, csem, zsem1, zrec1, zsem2, zrec2, ssem, rsem, asem, bsem, hello, above,
 ):
     n_sx, n_sy, n_row = sizes
@@ -136,8 +136,6 @@
     (y_down, y_up), x_first = y_copies(ys, yr, 0), x_copies(xs, xr, 2)
     (y_down2, y_up2), x_second = y_copies(ys2, yr2, 4), x_copies(xs2, xr2, 6)
 
-    pl.semaphore_wait(barrier, 2 + sum(c.astype(jnp.int32) for c in (has_prev, has_next, has_left)))
-    only(has_left, functools.partial(pl.semaphore_signal, above, inc=1, device_id=to_left, device_id_type=MESH))
     waits_long = has_right & (my_sy == n_sy // 2 - 1)
     waits_short = has_right & (my_sy != n_sy // 2 - 1)
 
@@ -194,6 +192,8 @@
         at = pl.ds(SUB * g, SUB)
         ys[0, 0, at, :], ys[1, 0, at, :] = faces(au, g)
         ys[0, 1, at, :], ys[1, 1, at, :] = faces(ad, g)
+    pl.semaphore_wait(barrier, 2 + sum(c.astype(jnp.int32) for c in (has_prev, has_next, has_left)))
+    only(has_left, functools.partial(pl.semaphore_signal, above, inc=1, device_id=to_left, device_id_type=MESH))
     start(y_down)
 
     def meet_above(cond):
@@ -417,48 +417,23 @@
 
     arrive(x_second)
     x_faces(lambda s, at: xs2[s, at, :], lambda s, at: xr2[s, at, :])
+
+    def brims_f(z0, carry, parity):
+        for xb, side, at_row in ((0, 0, 0), (blocks - 1, 1, SUB - 1)):
+            v = f[z0, rows(xb), :]
+            f[z0, rows(xb), :] = jnp.where(sub == at_row, v + fx[side, pl.ds(z0, SUB, stride=0), :], v)
+        return carry
+
+    sweep(0, depth // SUB, SUB, brims_f, 0)
+    for p in range(PARTS):
+        arrive(z_second(p))
     arrive(y_up2)
     arrive(y_down2)
     packed2, _ = y_faces(lambda s, at: ys2[s, at, :], lambda s, at: yr2[s, at, :])
-
-    def march(z0, carry, parity):
-        through, w0, w1 = [list(c) for c in carry]
-        for xb in range(blocks):
-            v = with_faces(f[z0, rows(xb), :], packed2, z0, parity, xb)
-            f[z0, rows(xb), :] = v
-            a, first, second = opaque(v, lab[z0 + 1, rows(xb), :])
-            w = through[xb] * a
-            through[xb] = through[xb] - w
-            w0[xb] = w0[xb] + jnp.where(first, w, 0.0)
-            w1[xb] = w1[xb] + jnp.where(second, w, 0.0)
-        return tuple(tuple(c) for c in (through, w0, w1))
-
-    state = sweep(1, (depth - 2) // MARCH, MARCH, march, ((one,) * blocks,) + ((zero,) * blocks,) * 2)
-    for i in range(3):
-        for xb in range(blocks):
-            mid[i, rows(xb), :] = state[i][xb]
-    for z0, _, parity in outer:
-        for xb in range(blocks):
-            f[z0, rows(xb), :] = with_faces(f[z0, rows(xb), :], packed2, z0, parity, xb)
+    for p in (0, 1):
+        for g in range(groups):
+            turn[p, pl.ds(SUB * g, SUB), :] = packed2[p][g]
     load_p.wait()
-
-    for p in range(PARTS):
-        arrive(z_second(p))
-    for xb in range(blocks):
-        at = rows(xb)
-        ends = []
-        for z0, ghost, parity in outer:
-            fz = flux(d[z0 + 1, at, :], d[ghost, at, :], h[ghost, at, :], h[z0 + 1, at, :])
-            v = f[z0, at, :] + fz
-            f[z0, at, :] = v
-            ends.append(opaque(v, lab[z0 + 1, at, :]))
-        (a, fa, fb), (b, ga, gb) = ends
-        clear_a = 1.0 - a
-        through = clear_a * mid[0, at, :]
-        w = through * b
-        ib[xb, 0] = jnp.where(fa, a, 0.0) + clear_a * mid[1, at, :] + jnp.where(ga, w, 0.0)
-        ib[xb, 1] = jnp.where(fb, a, 0.0) + clear_a * mid[2, at, :] + jnp.where(gb, w, 0.0)
-        ib[xb, 2] = through - w
 
     def hand(o):
         dest = lax.rem(me + o, n_row)
@@ -467,11 +442,56 @@
             device_id={"row": dest}, device_id_type=MESH,
         )
 
+    def march(dests):
+        places = []
+        for dest in dests:
+            at = pl.ds(pl.multiple_of(dest * SUB, SUB), SUB)
+            group = pl.ds(pl.multiple_of(dest // per_group * SUB, SUB), SUB)
+            sides = [turn[parity, group, :] for parity in (0, 1)]
+            places.append((at, sides, LANES - lax.rem(dest, per_group) * depth))
+
+        def warm(chunk):
+            got = {}
+            for z0 in chunk:
+                for i, (at, sides, m) in enumerate(places):
+                    v = f[z0, at, :]
+                    for edge_z, ghost in ((0, 0), (depth - 1, depth + 1)):
+                        if z0 == edge_z:
+                            v = v + flux(d[z0 + 1, at, :], d[ghost, at, :], h[ghost, at, :], h[z0 + 1, at, :])
+                    got[z0, i] = jnp.where(at_ends, v + pltpu.roll(sides[z0 % 2], (m - z0) & (LANES - 1), 1), v)
+            return got
+
+        states = [(None, zero, zero)] * len(dests)
+        steps = [range(k, k + MARCH) for k in range(0, depth, MARCH)]
+        ahead = warm(steps[0])
+        for k, chunk in enumerate(steps):
+            now, ahead = ahead, warm(steps[k + 1]) if k + 1 < len(steps) else None
+            for (z0, i), v in now.items():
+                f[z0, places[i][0], :] = v
+            for (z0, i), v in now.items():
+                through, w0, w1 = states[i]
+                w, first, second = opaque(v, lab[z0 + 1, places[i][0], :])
+                if through is None:
+                    through = 1.0 - w
+                else:
+                    w = through * w
+                    through = through - w
+                w0 = w0 + jnp.where(first, w, 0.0)
+                w1 = w1 + jnp.where(second, w, 0.0)
+                states[i] = (through, w0, w1)
+        for dest, (through, w0, w1) in zip(dests, states):
+            ib[dest, 0] = w0
+            ib[dest, 1] = w1
+            ib[dest, 2] = through
+
     greet(1, 4, "wait")
     half = n_row // 2
-    order = sorted(range(1, n_row), key=lambda o: abs(o - half))
-    for o in order:
-        hand(o).start()
+    order = [half + 1, half - 1, half] + [o for k in range(1, half - 1) for o in (n_row - k, k)] + [0]
+    for k in range(0, n_row, 2):
+        march([lax.rem(me + o, n_row) for o in order[k : k + 2]])
+        for o in order[k : k + 2]:
+            if o:
+                hand(o).start()
     rb[me] = ib[me]
 
     for s in range(n_row):
@@ -493,7 +513,7 @@
         pic_ref[c] = w0 * tint[0, c] + w1 * tint[1, c] + w2 * tint[2, c]
     pic_ref[3] = blocked
 
-    for o in order:
+    for o in range(1, n_row):
         hand(o).wait_send()
     for p in range(PARTS):
         left_here(z_first(p))
@@ -547,7 +567,7 @@
                 pltpu.VMEM((2, 2, side, tall), f32),
                 pltpu.VMEM((2, side, tall), f32),
                 pltpu.VMEM((2, side, tall), f32),
-                pltpu.VMEM((3, wide, tall), f32),
+                pltpu.VMEM((2, side, tall), f32),
                 pltpu.VMEM((n_row, 3, wide // n_row, tall), f32),
                 pltpu.VMEM((n_row, 3, wide // n_row, tall), f32),
                 pltpu.SMEM((3,), f32),

time: 24.5 us -> 23.5 us (0.959)
  Pallas kernels: 23.8 us -> 22.8 us
    pallas_call x1, Pallas kernels: 22.8 us -> 21.8 us  [per_device(): pl.pallas_call(functools.partial(kernel, sizes), out_shape=results, in_sp...]
where the time goes in v7:
time: 23.5 us; the launch traced here: 23.4 us
  Pallas kernels  22.8 us (97%)
  between operations  0.64 us (3%)
    pallas_call x1, Pallas kernels, per_device(): pl.pallas_call(functools.partial(kernel, sizes), out_shape=results, in_sp...  21.8 us
    pallas_call x1, Pallas kernels, per_device(): pl.pallas_call(deliver, out_shape=results, in_specs=[near, near], out_spe...  0.99 us

profile of v7, /device:TPU:64, one launch (start us, length us, event | category | flops | bytes accessed | tf_op | source)
XLA Modules:
  0.0 23.4 jit_solution(173546928881621445)
XLA Ops:
  0.6 21.8 %shard_map.68 = (f32[32,64,128]{2,1,0:T(8,128)S(1)}, f32[4,8,128]{2,1,0:T(8,128)S(1)}) custom-call(f32[32,64,128]{2,1,0:T(8,128)} %t_hbm.1, s32[32,64,128]{2,1,0:T(8,128)} %lab_hbm.1, f32[3]{0:T(128)} %coef_hbm.1, f32[3]{0:T(128)} %thick_hbm.1, f32[3,3]{1,0:T(4,128)} %tint_hbm.1), custom_call_target="tpu_custom_call" | custom-call | tf_op jit(solution)/shard_map/pallas_call | solution.py:549
  22.4 1.0 %shard_map.69 = (f32[32,64,128]{2,1,0:T(8,128)}, f32[4,8,128]{2,1,0:T(8,128)}) custom-call(f32[32,64,128]{2,1,0:T(8,128)S(1)} %get-tuple-element.4.f, f32[4,8,128]{2,1,0:T(8,128)S(1)} %get-tuple-element.5.pic), custom_call_target="tpu_custom_call" | custom-call | tf_op jit(solution)/shard_map/pallas_call | solution.py:596

commit v8 on v7

--- a/solution.py
+++ b/solution.py
@@ -107,7 +107,7 @@
     def z_first(p):
         at = pl.ds(SUB * per_part * p, SUB * per_part)
         got = []
-        for i, (src, dst) in enumerate(((t_hbm, u), (lab_hbm, lab))):
+        for i, (src, dst) in enumerate(((lab_hbm, lab), (t_hbm, u))):
             got.append((remote(src.at[depth - 1, at], dst.at[0, at], zsem1.at[0, i, p], zrec1.at[0, i, p], to_next),
                         has_next, has_prev))
             got.append((remote(src.at[0, at], dst.at[depth + 1, at], zsem1.at[1, i, p], zrec1.at[1, i, p], to_prev),
@@ -136,6 +136,11 @@
     (y_down, y_up), x_first = y_copies(ys, yr, 0), x_copies(xs, xr, 2)
     (y_down2, y_up2), x_second = y_copies(ys2, yr2, 4), x_copies(xs2, xr2, 6)
 
+    def enter():
+        pl.semaphore_wait(barrier, 2 + sum(c.astype(jnp.int32) for c in (has_prev, has_next, has_left)))
+        only(has_left, functools.partial(pl.semaphore_signal, above, inc=1, device_id=to_left, device_id_type=MESH))
+
+    pl.when(my_sy == n_sy // 2)(enter)
     waits_long = has_right & (my_sy == n_sy // 2 - 1)
     waits_short = has_right & (my_sy != n_sy // 2 - 1)
 
@@ -192,8 +197,7 @@
         at = pl.ds(SUB * g, SUB)
         ys[0, 0, at, :], ys[1, 0, at, :] = faces(au, g)
         ys[0, 1, at, :], ys[1, 1, at, :] = faces(ad, g)
-    pl.semaphore_wait(barrier, 2 + sum(c.astype(jnp.int32) for c in (has_prev, has_next, has_left)))
-    only(has_left, functools.partial(pl.semaphore_signal, above, inc=1, device_id=to_left, device_id_type=MESH))
+    pl.when(my_sy != n_sy // 2)(enter)
     start(y_down)
 
     def meet_above(cond):

time: 23.5 us -> 23.4 us (level)
  no operation moved by 1% of the time
where the time goes in v8:
time: 23.4 us; the launch traced here: 23.3 us
  Pallas kernels  22.7 us (97%)
  between operations  0.64 us (3%)
    pallas_call x1, Pallas kernels, per_device(): pl.pallas_call(functools.partial(kernel, sizes), out_shape=results, in_sp...  21.7 us
    pallas_call x1, Pallas kernels, per_device(): pl.pallas_call(deliver, out_shape=results, in_specs=[near, near], out_spe...  0.99 us

profile of v8, /device:TPU:64, one launch (start us, length us, event | category | flops | bytes accessed | tf_op | source)
XLA Modules:
  0.0 23.3 jit_solution(16841628876454499530)
XLA Ops:
  0.6 21.7 %shard_map.68 = (f32[32,64,128]{2,1,0:T(8,128)S(1)}, f32[4,8,128]{2,1,0:T(8,128)S(1)}) custom-call(f32[32,64,128]{2,1,0:T(8,128)} %t_hbm.1, s32[32,64,128]{2,1,0:T(8,128)} %lab_hbm.1, f32[3]{0:T(128)} %coef_hbm.1, f32[3]{0:T(128)} %thick_hbm.1, f32[3,3]{1,0:T(4,128)} %tint_hbm.1), custom_call_target="tpu_custom_call" | custom-call | tf_op jit(solution)/shard_map/pallas_call | solution.py:553
  22.3 1.0 %shard_map.69 = (f32[32,64,128]{2,1,0:T(8,128)}, f32[4,8,128]{2,1,0:T(8,128)}) custom-call(f32[32,64,128]{2,1,0:T(8,128)S(1)} %get-tuple-element.4.f, f32[4,8,128]{2,1,0:T(8,128)S(1)} %get-tuple-element.5.pic), custom_call_target="tpu_custom_call" | custom-call | tf_op jit(solution)/shard_map/pallas_call | solution.py:600

commit v9 on v8

--- a/solution.py
+++ b/solution.py
@@ -527,12 +527,16 @@
 
 
 def deliver(f, pic, out, out_pic, sem):
-    a = pltpu.make_async_copy(f, out, sem.at[0])
-    b = pltpu.make_async_copy(pic, out_pic, sem.at[1])
-    a.start()
-    b.start()
-    a.wait()
-    b.wait()
+    half = f.shape[0] // 2
+    copies = [
+        pltpu.make_async_copy(f.at[pl.ds(half * i, half)], out.at[pl.ds(half * i, half)], sem.at[i]) for i in (0, 1)
+    ]
+    last = pltpu.make_async_copy(pic, out_pic, sem.at[2])
+    copies[0].start(priority=0)
+    copies[1].start(priority=1)
+    last.start(priority=1)
+    for copy in copies + [last]:
+        copy.wait()
 
 
 def solution(mesh):
@@ -602,7 +606,7 @@
             out_shape=results,
             in_specs=[near, near],
             out_specs=(anywhere, anywhere),
-            scratch_shapes=[pltpu.SemaphoreType.DMA((2,))],
+            scratch_shapes=[pltpu.SemaphoreType.DMA((3,))],
             compiler_params=pltpu.CompilerParams(vmem_limit_bytes=VMEM_LIMIT),
         )(f, pic)
 

time: 23.4 us -> 23.4 us (level)
  no operation moved by 1% of the time
where the time goes in v9:
time: 23.4 us; the launch traced here: 23.3 us
  Pallas kernels  22.7 us (97%)
  between operations  0.64 us (3%)
    pallas_call x1, Pallas kernels, per_device(): pl.pallas_call(functools.partial(kernel, sizes), out_shape=results, in_sp...  21.7 us
    pallas_call x1, Pallas kernels, per_device(): pl.pallas_call(deliver, out_shape=results, in_specs=[near, near], out_spe...  1 us

profile of v9, /device:TPU:64, one launch (start us, length us, event | category | flops | bytes accessed | tf_op | source)
XLA Modules:
  0.0 23.3 jit_solution(4210370778124440706)
XLA Ops:
  0.6 21.7 %shard_map.68 = (f32[32,64,128]{2,1,0:T(8,128)S(1)}, f32[4,8,128]{2,1,0:T(8,128)S(1)}) custom-call(f32[32,64,128]{2,1,0:T(8,128)} %t_hbm.1, s32[32,64,128]{2,1,0:T(8,128)} %lab_hbm.1, f32[3]{0:T(128)} %coef_hbm.1, f32[3]{0:T(128)} %thick_hbm.1, f32[3,3]{1,0:T(4,128)} %tint_hbm.1), custom_call_target="tpu_custom_call" | custom-call | tf_op jit(solution)/shard_map/pallas_call | solution.py:557
  22.3 1.0 %shard_map.69 = (f32[32,64,128]{2,1,0:T(8,128)}, f32[4,8,128]{2,1,0:T(8,128)}) custom-call(f32[32,64,128]{2,1,0:T(8,128)S(1)} %get-tuple-element.4.f, f32[4,8,128]{2,1,0:T(8,128)S(1)} %get-tuple-element.5.pic), custom_call_target="tpu_custom_call" | custom-call | tf_op jit(solution)/shard_map/pallas_call | solution.py:604

commit v10 on v8

--- a/solution.py
+++ b/solution.py
@@ -42,31 +42,31 @@
     load_c = pltpu.make_async_copy(coef_hbm, coef, csem.at[0])
     load_k = pltpu.make_async_copy(thick_hbm, thick, csem.at[1])
     load_p = pltpu.make_async_copy(tint_hbm, tint, csem.at[2])
+    sx_next = lax.rem(my_sx + 1, n_sx)
+    sx_prev = lax.rem(my_sx + n_sx - 1, n_sx)
+    to_next, to_prev = {"row": me + 1}, {"row": me - 1}
+    to_right, to_left = {"sy": my_sy + 1}, {"sy": my_sy - 1}
+    to_up, to_down = {"sx": sx_next}, {"sx": sx_prev}
+
+    def only(cond, act):
+        if cond is None:
+            act()
+        else:
+            pl.when(cond)(act)
+
+    barrier = pltpu.get_barrier_semaphore()
+    near = (
+        (has_prev, to_prev), (has_next, to_next), (has_right, to_right), (None, to_up), (None, to_down),
+    )
+    for there, where in near:
+        only(there, functools.partial(pl.semaphore_signal, barrier, inc=1, device_id=where, device_id_type=MESH))
+
     load_c.start()
     for j in range(chunks):
         for copy in load(j):
             copy.start()
     load_k.start()
     load_p.start()
-
-    sx_next = lax.rem(my_sx + 1, n_sx)
-    sx_prev = lax.rem(my_sx + n_sx - 1, n_sx)
-    to_next, to_prev = {"row": me + 1}, {"row": me - 1}
-    to_right, to_left = {"sy": my_sy + 1}, {"sy": my_sy - 1}
-    to_up, to_down = {"sx": sx_next}, {"sx": sx_prev}
-
-    def only(cond, act):
-        if cond is None:
-            act()
-        else:
-            pl.when(cond)(act)
-
-    barrier = pltpu.get_barrier_semaphore()
-    near = (
-        (has_prev, to_prev), (has_next, to_next), (has_right, to_right), (None, to_up), (None, to_down),
-    )
-    for there, where in near:
-        only(there, functools.partial(pl.semaphore_signal, barrier, inc=1, device_id=where, device_id_type=MESH))
 
     lane = lax.broadcasted_iota(jnp.int32, (SUB, LANES), 1)
     sub = lax.broadcasted_iota(jnp.int32, (SUB, LANES), 0)
@@ -498,6 +498,7 @@
                 hand(o).start()
     rb[me] = ib[me]
 
+    through, w0, w1 = one, zero, zero
     for s in range(n_row):
         @pl.when(me != s)
         def _():
@@ -506,8 +507,6 @@
                 device_id={"row": s}, device_id_type=MESH,
             ).wait_recv()
 
-    through, w0, w1 = one, zero, zero
-    for s in range(n_row):
         w0 = w0 + through * rb[s, 0]
         w1 = w1 + through * rb[s, 1]
         through = through * rb[s, 2]

time: 23.4 us -> 23.5 us (level)
  no operation moved by 1% of the time
where the time goes in v10:
time: 23.5 us; the launch traced here: 23.4 us
  Pallas kernels  22.7 us (97%)
  between operations  0.64 us (3%)
    pallas_call x1, Pallas kernels, per_device(): pl.pallas_call(functools.partial(kernel, sizes), out_shape=results, in_sp...  21.7 us
    pallas_call x1, Pallas kernels, per_device(): pl.pallas_call(deliver, out_shape=results, in_specs=[near, near], out_spe...  0.99 us

profile of v10, /device:TPU:64, one launch (start us, length us, event | category | flops | bytes accessed | tf_op | source)
XLA Modules:
  0.0 23.4 jit_solution(5291981493820278089)
XLA Ops:
  0.6 21.7 %shard_map.68 = (f32[32,64,128]{2,1,0:T(8,128)S(1)}, f32[4,8,128]{2,1,0:T(8,128)S(1)}) custom-call(f32[32,64,128]{2,1,0:T(8,128)} %t_hbm.1, s32[32,64,128]{2,1,0:T(8,128)} %lab_hbm.1, f32[3]{0:T(128)} %coef_hbm.1, f32[3]{0:T(128)} %thick_hbm.1, f32[3,3]{1,0:T(4,128)} %tint_hbm.1), custom_call_target="tpu_custom_call" | custom-call | tf_op jit(solution)/shard_map/pallas_call | solution.py:552
  22.4 1.0 %shard_map.69 = (f32[32,64,128]{2,1,0:T(8,128)}, f32[4,8,128]{2,1,0:T(8,128)}) custom-call(f32[32,64,128]{2,1,0:T(8,128)S(1)} %get-tuple-element.4.f, f32[4,8,128]{2,1,0:T(8,128)S(1)} %get-tuple-element.5.pic), custom_call_target="tpu_custom_call" | custom-call | tf_op jit(solution)/shard_map/pallas_call | solution.py:599
